TPU v7x, 32 devices: a whole 2x2x4 slice. The times are simulated.
32 devices in a mesh: tiles: 8 (over z, y), rhs: 4 (over x, core).
Axes of the slice: x: 2, y: 2, z: 4, core: 2. Of those that a mesh axis runs over, the one named last changes fastest.
Arguments:
- rhs_rows: bfloat16 [256, 8192], P('rhs', 'tiles'), may hold values from -6 to 6
- diag_inverse: bfloat16 [8192, 1024], P('tiles', 'rhs'), may hold values from -0.0625 to 0.5625
- u_factors: bfloat16 [8, 7, 1024, 128], P('tiles'), may hold values from -0.1875 to 0.1875
- v_factors: bfloat16 [8, 7, 1024, 128], P('tiles'), may hold values from -0.1875 to 0.1875
- tile_rows: int32 [8, 7], P('tiles'), may hold values from 0 to 7, as said below
- tile_ranks: int32 [8, 7], P('tiles'), may hold values from 16 to 128
- point_coords: float32 [8, 8192], P(None, 'tiles'), may hold values from 0 to 1
- cand_coords: float32 [8, 128], P(None, 'rhs'), may hold values from 0 to 1
- owner: int32 [128], P('rhs'), may hold values from 0 to 7, as said below
Outputs:
- solution: bfloat16 [256, 8192], P('rhs', 'tiles')
- predictions: float32 [128, 256], P(('tiles', 'rhs'))
Inputs may be any that keep to these rules, and one draw needn't show every extreme that they name: Each tile column lists 7 distinct tile rows, none equal to itself; for each slot k, tile_rows[., k] is a permutation of the tile rows. `owner`: in each group of 32 consecutive candidates every tile owns exactly 4.
All inputs are finite; a program needn't handle non-finite values.
Results may differ from a plain program's by a relative error of at most 0.008.
Values may be sent and summed in bfloat16 or wider, within the bound.
No kernel may reach another device: no remote copies, remote signals or barrier semaphores. Data moves between devices by JAX's collectives and lax.ppermute only.
A program may use at most 64 MiB of HBM per device.

v0:
```python
import math

import jax
import jax.numpy as jnp
from jax import lax
from jax.sharding import PartitionSpec as P

ITERS = 2


def kernel_block(cand, cand_sq, points, amplitude):
    point_sq = jnp.sum(points * points, 0)
    inner_products = lax.dot_general(
        cand, points, (((0,), (0,)), ((), ())), precision=lax.Precision.HIGHEST
    )
    dist_sq = cand_sq[:, None] + point_sq[None, :] - 2.0 * inner_products
    return (jnp.exp(-2.0 * dist_sq) * amplitude).astype(jnp.bfloat16)


def per_device(
    rhs_rows,
    diag_inverse,
    u_factors,
    v_factors,
    tile_rows,
    tile_ranks,
    point_coords,
    cand_coords,
    owner,
):
    tiles_count = lax.axis_size("tiles")
    tile_here = lax.axis_index("tiles")
    u_slots = u_factors[0]
    v_slots = v_factors[0]
    width = u_slots.shape[2]
    slot_count = u_slots.shape[0]
    rank_mask = (
        lax.broadcasted_iota(jnp.int32, (slot_count, width), 1) < tile_ranks[0][:, None]
    ).astype(jnp.bfloat16)
    peer_ids = jnp.arange(tiles_count, dtype=jnp.int32)
    all_rows = lax.all_gather(tile_rows, "tiles", axis=0, tiled=True)
    slot_range = jnp.arange(slot_count, dtype=jnp.int32)
    column_ids = jnp.broadcast_to(peer_ids[:, None], all_rows.shape)
    all_sources = (
        jnp.zeros(all_rows.shape, jnp.int32).at[all_rows, slot_range[None, :]].set(column_ids)
    )
    sources_here = lax.dynamic_slice_in_dim(all_sources, tile_here, 1, 0)[0]
    to_rows = (peer_ids[:, None] == tile_rows[0][None, :]).astype(jnp.bfloat16)
    to_cols = (peer_ids[:, None] == sources_here[None, :]).astype(jnp.bfloat16)
    whole_inverse = lax.all_gather(diag_inverse, "rhs", axis=1, tiled=True)

    def precondition(resid):
        return jnp.dot(resid, whole_inverse, preferred_element_type=jnp.float32).astype(
            jnp.bfloat16
        )

    iterate = precondition(rhs_rows)
    for sweep in range(ITERS):
        lower = jnp.einsum("cb,kbr->kcr", iterate, v_slots, preferred_element_type=jnp.float32)
        lower = (lower * rank_mask[:, None, :]).astype(jnp.bfloat16)
        upper = jnp.einsum(
            "cb,kbr->kcr", iterate, u_slots, preferred_element_type=jnp.float32
        ).astype(jnp.bfloat16)
        send_lower = jnp.einsum(
            "nk,kcr->ncr", to_rows, lower, preferred_element_type=jnp.float32
        ).astype(jnp.bfloat16)
        send_upper = jnp.einsum(
            "nk,kcr->ncr", to_cols, upper, preferred_element_type=jnp.float32
        ).astype(jnp.bfloat16)
        from_picked = jnp.einsum(
            "nk,ncr->kcr",
            to_cols,
            lax.all_to_all(send_lower, "tiles", split_axis=0, concat_axis=0, tiled=True),
            preferred_element_type=jnp.float32,
        ).astype(jnp.bfloat16)
        first = jnp.einsum("kcr,kbr->cb", from_picked, u_slots, preferred_element_type=jnp.float32)
        picked = jnp.einsum(
            "nk,ncr->kcr",
            to_rows,
            lax.all_to_all(send_upper, "tiles", split_axis=0, concat_axis=0, tiled=True),
            preferred_element_type=jnp.float32,
        ).astype(jnp.bfloat16)
        picked = picked * rank_mask[:, None, :]
        second = jnp.einsum("kcr,kbr->cb", picked, v_slots, preferred_element_type=jnp.float32)
        resid = (rhs_rows.astype(jnp.float32) - (first + second)).astype(jnp.bfloat16)
        iterate = precondition(resid)
    block_len = u_slots.shape[1]
    amplitude = 4.0 / math.sqrt(block_len * tiles_count)
    cand_sq = jnp.sum(cand_coords * cand_coords, 0)
    cross = kernel_block(cand_coords, cand_sq, point_coords, amplitude)
    partial_values = lax.dot_general(
        cross,
        lax.all_gather(iterate, "rhs", axis=0, tiled=True),
        (((1,), (1,)), ((), ())),
        preferred_element_type=jnp.float32,
    )
    group_len = owner.shape[0]
    owned = group_len // tiles_count
    owner_hot = (owner[:, None] == peer_ids[None, :]).astype(jnp.int32)
    running = jnp.cumsum(owner_hot, axis=0)
    slot_of = owner * owned + jnp.sum(running * owner_hot, axis=1) - 1
    ordered = jnp.zeros_like(partial_values).at[slot_of].set(partial_values)
    summed = lax.psum(ordered, "tiles")
    owned_sums = lax.dynamic_slice_in_dim(summed, tile_here * owned, owned, 0)
    return (iterate, owned_sums)


def solution(mesh):
    in_specs = (
        P("rhs", "tiles"),
        P("tiles", "rhs"),
        P("tiles", None, None, None),
        P("tiles", None, None, None),
        P("tiles", None),
        P("tiles", None),
        P(None, "tiles"),
        P(None, "rhs"),
        P("rhs"),
    )
    out_specs = (P("rhs", "tiles"), P(("tiles", "rhs"), None))
    return jax.shard_map(
        per_device, mesh=mesh, in_specs=in_specs, out_specs=out_specs, check_vma=False
    )
```

profile of v0, /device:TPU:0, one launch (start us, length us, event | category | flops | bytes accessed | tf_op | source)
XLA Modules:
  0.0 142.5 jit_solution(6352598870871334731)
XLA Ops:
  7.2 0.0 copy-start
  7.2 0.0 all-gather.3.cloned.1.call-start
  7.2 0.7 all-gather.3.cloned.1.call-update
  7.9 22.5 %all-gather = s32[8,1,7]{2,1,0:T(1,128)S(1)} all-gather(s32[1,1,7]{2,1,0:T(1,128)} %bitcast.143), channel_id=1, replica_groups=mesh['tiles'=8,'rhs'=4] {'tiles'}, dimensions={0}, use_global_device_ids=true | all-gather | bytes 252 | tf_op jit(solution)/shard_map/all_gather | solution.py:41
  30.4 0.1 reshape.46
  30.5 0.1 reshape.48
  30.6 0.7 fusion.107
  31.3 0.1 reduce_window_sum.11
  31.4 0.0 copy-start.4
  31.4 3.5 %scatter_fusion = s32[8,7]{1,0:T(8,128)S(1)} fusion(s32[8,7]{1,0:T(8,128)S(1)} %broadcast.30, s32[56]{0:T(128)S(1)} %reshape.46, s32[56]{0:T(128)S(1)} %reshape.48), kind=kCustom, calls=%fused_computation | custom fusion | bytes 1120 | tf_op jit(solution)/shard_map/scatter | solution.py:45
  35.0 0.2 select_reduce_fusion
  35.2 0.1 fusion.134
  35.2 0.3 fusion.90
  35.6 0.0 all-gather.3.cloned.1.call-done
  35.6 2.2 %fusion.71 = bf16[64,1024,1]{1,0,2:T(8,128)(2,1)S(1)} fusion(bf16[64,1024]{1,0:T(8,128)(2,1)S(1)} %copy-done.2, bf16[1024,1024]{1,0:T(8,128)(2,1)} %all-gather.3.cloned.1.call-done), kind=kOutput, calls=%fused_computation.46 | convolution fusion | flops 134283264 | bytes 2359296 | tf_op jit(solution)/shard_map/dot_general | solution.py:53
  37.9 0.4 fusion.87
  38.3 0.2 convolution_convert_fusion.8
  38.5 0.7 copy.30
  39.2 5.0 %all-to-all-start.1 = ((bf16[8,64,128]{2,1,0:T(8,128)(2,1)}), bf16[8,64,128]{2,1,0:T(8,128)(2,1)S(1)}, u32[]{:S(2)}, u32[]{:S(2)}) async-start(bf16[8,64,128]{2,1,0:T(8,128)(2,1)} %copy.30), calls=%async_computation.1 | async-start | bytes 262144 | tf_op jit(solution)/shard_map/all_to_all | solution.py:80
  44.2 0.4 fusion.78
  44.6 0.3 convolution_convert_fusion.10
  44.9 0.7 copy.25
  45.6 6.0 %all-to-all-done.1 = bf16[8,64,128]{2,1,0:T(8,128)(2,1)S(1)} async-done(((bf16[8,64,128]{2,1,0:T(8,128)(2,1)}), bf16[8,64,128]{2,1,0:T(8,128)(2,1)S(1)}, u32[]{:S(2)}, u32[]{:S(2)}) %all-to-all-start.1) | async-done | bytes 131104 | tf_op jit(solution)/shard_map/all_to_all | solution.py:80
  51.6 3.4 %all-to-all-start = ((bf16[8,64,128]{2,1,0:T(8,128)(2,1)}), bf16[8,64,128]{2,1,0:T(8,128)(2,1)S(1)}, u32[]{:S(2)}, u32[]{:S(2)}) async-start(bf16[8,64,128]{2,1,0:T(8,128)(2,1)} %copy.25), calls=%async_computation | async-start | bytes 262144 | tf_op jit(solution)/shard_map/all_to_all | solution.py:73
  54.9 0.2 fusion.72
  55.2 0.7 fusion.16
  55.9 6.4 %all-to-all-done = bf16[8,64,128]{2,1,0:T(8,128)(2,1)S(1)} async-done(((bf16[8,64,128]{2,1,0:T(8,128)(2,1)}), bf16[8,64,128]{2,1,0:T(8,128)(2,1)S(1)}, u32[]{:S(2)}, u32[]{:S(2)}) %all-to-all-start) | async-done | bytes 131104 | tf_op jit(solution)/shard_map/all_to_all | solution.py:73
  62.2 0.2 convolution_convert_fusion.9
  62.5 3.2 %fusion.68 = bf16[64,1024,1]{1,0,2:T(8,128)(2,1)S(1)} fusion(bf16[1024,1024]{1,0:T(8,128)(2,1)} %all-gather.3.cloned.1.call-done, f32[64,1024]{1,0:T(8,128)S(1)} %fusion.16, bf16[1,7,1024,128]{3,2,1,0:T(8,128)(2,1)} %param.11, bf16[64,1024]{1,0:T(8,128)(2,1)S(1)} %copy-done.2, bf16[7,64,128]{2,0,1:T(8,128)(2,1)S(1)} %convolution_convert_fusion.9), kind=kOutput, calls=%fused_computation.45 | convolution fusion | flops 251985920 | bytes 4571136 | tf_op jit(solution)/shard_map/dot_general | solution.py:53
  65.7 1.9 %fusion.84 = bf16[7,64,128]{2,1,0:T(8,128)(2,1)S(1)} fusion(bf16[64,1024,1]{1,0,2:T(8,128)(2,1)S(1)} %fusion.68, bf16[1,7,1024,128]{3,2,1,0:T(8,128)(2,1)} %param.11), kind=kOutput, calls=%fused_computation.56 | convolution fusion | flops 117497856 | bytes 2080768 | tf_op jit(solution)/shard_map/cb,kbr->kcr/dot_general | solution.py:61
  67.6 0.4 fusion.81
  68.0 0.2 convolution_convert_fusion.4
  68.2 0.7 copy.40
  68.9 3.4 %all-to-all-start.3 = ((bf16[8,64,128]{2,1,0:T(8,128)(2,1)}), bf16[8,64,128]{2,1,0:T(8,128)(2,1)S(1)}, u32[]{:S(2)}, u32[]{:S(2)}) async-start(bf16[8,64,128]{2,1,0:T(8,128)(2,1)} %copy.40), calls=%async_computation.3 | async-start | bytes 262144 | tf_op jit(solution)/shard_map/all_to_all | solution.py:80
  72.3 0.3 convolution_convert_fusion.6
  72.6 0.7 copy.35
  73.3 6.3 %all-to-all-done.3 = bf16[8,64,128]{2,1,0:T(8,128)(2,1)S(1)} async-done(((bf16[8,64,128]{2,1,0:T(8,128)(2,1)}), bf16[8,64,128]{2,1,0:T(8,128)(2,1)S(1)}, u32[]{:S(2)}, u32[]{:S(2)}) %all-to-all-start.3) | async-done | bytes 131104 | tf_op jit(solution)/shard_map/all_to_all | solution.py:80
  79.6 3.4 %all-to-all-start.2 = ((bf16[8,64,128]{2,1,0:T(8,128)(2,1)}), bf16[8,64,128]{2,1,0:T(8,128)(2,1)S(1)}, u32[]{:S(2)}, u32[]{:S(2)}) async-start(bf16[8,64,128]{2,1,0:T(8,128)(2,1)} %copy.35), calls=%async_computation.2 | async-start | bytes 262144 | tf_op jit(solution)/shard_map/all_to_all | solution.py:73
  82.9 0.2 fusion.73
  83.2 0.7 fusion.19
  83.9 6.4 %all-to-all-done.2 = bf16[8,64,128]{2,1,0:T(8,128)(2,1)S(1)} async-done(((bf16[8,64,128]{2,1,0:T(8,128)(2,1)}), bf16[8,64,128]{2,1,0:T(8,128)(2,1)S(1)}, u32[]{:S(2)}, u32[]{:S(2)}) %all-to-all-start.2) | async-done | bytes 131104 | tf_op jit(solution)/shard_map/all_to_all | solution.py:73
  90.2 0.2 convolution_convert_fusion.5
  90.5 3.2 %convolution_convert_fusion = bf16[64,1024]{1,0:T(8,128)(2,1)S(1)} fusion(bf16[1024,1024]{1,0:T(8,128)(2,1)} %all-gather.3.cloned.1.call-done, f32[64,1024]{1,0:T(8,128)S(1)} %fusion.19, bf16[1,7,1024,128]{3,2,1,0:T(8,128)(2,1)} %param.11, bf16[64,1024]{1,0:T(8,128)(2,1)S(1)} %copy-done.2, bf16[7,64,128]{2,0,1:T(8,128)(2,1)S(1)} %convolution_convert_fusion.5), kind=kOutput, calls=%fused_computation.30 | convolution fusion | flops 251985920 | bytes 4571136 | tf_op jit(solution)/shard_map/dot_general | solution.py:53
  93.7 6.5 %all_gather.11 = bf16[256,1024]{1,0:T(8,128)(2,1)S(1)} all-gather(bf16[64,1024]{1,0:T(8,128)(2,1)S(1)} %convolution_convert_fusion), channel_id=1, replica_groups=mesh['tiles'=8,'rhs'=4] {'rhs'}, dimensions={0}, use_global_device_ids=true | all-gather | bytes 655360 | tf_op jit(solution)/shard_map/all_gather | solution.py:93
  100.2 0.2 fusion.135
  100.4 0.7 scatter_custom_fusion.1
  101.2 33.9 %psum.7 = f32[32,256]{1,0:T(8,128)S(1)} all-reduce(f32[32,256]{1,0:T(8,128)S(1)} %scatter_custom_fusion.1), channel_id=1, replica_groups=mesh['tiles'=8,'rhs'=4] {'tiles'}, use_global_device_ids=true, to_apply=%region_6.7 | all-reduce | flops 8192 | bytes 65536 | tf_op jit(solution)/shard_map/psum | solution.py:103
  135.1 0.6 constant_dynamic-slice_fusion
  (23 shorter events, 0.1 us)
Async XLA Ops:
  7.2 37.0 %copy-start = (bf16[1,7,1024,128]{3,2,1,0:T(8,128)(2,1)S(1)}, bf16[1,7,1024,128]{3,2,1,0:T(8,128)(2,1)}, u32[]{:S(2)}) copy-start(bf16[1,7,1024,128]{3,2,1,0:T(8,128)(2,1)} %param.12) | copy-start | bytes 5505028
  7.2 28.4 %all-gather.3.cloned.1.call-start = ((), (), s32[]{:S(2)}) async-start(), calls=%async_computation.4 | async-start | bytes 2621440 | tf_op jit(solution)/shard_map/all_gather | solution.py:50
  31.4 3.5 %copy-start.6 = (f32[8,32]{1,0:T(8,128)S(1)}, f32[8,32]{1,0:T(8,128)}, u32[]{:S(2)}) copy-start(f32[8,32]{1,0:T(8,128)} %param.16) | copy-start | bytes 3076
  31.4 3.6 %copy-start.4 = (f32[8,1024]{1,0:T(8,128)S(1)}, f32[8,1024]{1,0:T(8,128)}, u32[]{:S(2)}) copy-start(f32[8,1024]{1,0:T(8,128)} %param.15) | copy-start | bytes 98308
  31.4 3.6 %copy-start.7 = (s32[32]{0:T(128)S(1)}, s32[32]{0:T(128)}, u32[]{:S(2)}) copy-start(s32[32]{0:T(128)} %param.17) | copy-start | bytes 388
  31.4 3.8 %copy-start.8 = (s32[1,7]{1,0:T(1,128)S(1)}, s32[1,7]{1,0:T(1,128)}, u32[]{:S(2)}) copy-start(s32[1,7]{1,0:T(1,128)} %param.14) | copy-start | bytes 88
  31.4 4.2 %copy-start.2 = (bf16[64,1024]{1,0:T(8,128)(2,1)S(1)}, bf16[64,1024]{1,0:T(8,128)(2,1)}, u32[]{:S(2)}) copy-start(bf16[64,1024]{1,0:T(8,128)(2,1)} %param.9) | copy-start | bytes 393220
  35.6 2.2 %copy-start.1 = (bf16[1,7,1024,128]{3,2,1,0:T(8,128)(2,1)S(1)}, bf16[1,7,1024,128]{3,2,1,0:T(8,128)(2,1)}, u32[]{:S(2)}) copy-start(bf16[1,7,1024,128]{3,2,1,0:T(8,128)(2,1)} %param.11) | copy-start | bytes 5505028
  38.3 6.3 %copy-start.5 = (s32[1,7]{1,0:T(1,128)S(1)}, s32[1,7]{1,0:T(1,128)}, u32[]{:S(2)}) copy-start(s32[1,7]{1,0:T(1,128)} %param.13) | copy-start | bytes 88
  39.2 12.4 %all-to-all-start.1 = ((bf16[8,64,128]{2,1,0:T(8,128)(2,1)}), bf16[8,64,128]{2,1,0:T(8,128)(2,1)S(1)}, u32[]{:S(2)}, u32[]{:S(2)}) async-start(bf16[8,64,128]{2,1,0:T(8,128)(2,1)} %copy.30), calls=%async_computation.1 | async-start | bytes 262144 | tf_op jit(solution)/shard_map/all_to_all | solution.py:80
  51.6 10.7 %all-to-all-start = ((bf16[8,64,128]{2,1,0:T(8,128)(2,1)}), bf16[8,64,128]{2,1,0:T(8,128)(2,1)S(1)}, u32[]{:S(2)}, u32[]{:S(2)}) async-start(bf16[8,64,128]{2,1,0:T(8,128)(2,1)} %copy.25), calls=%async_computation | async-start | bytes 262144 | tf_op jit(solution)/shard_map/all_to_all | solution.py:73
  68.9 10.7 %all-to-all-start.3 = ((bf16[8,64,128]{2,1,0:T(8,128)(2,1)}), bf16[8,64,128]{2,1,0:T(8,128)(2,1)S(1)}, u32[]{:S(2)}, u32[]{:S(2)}) async-start(bf16[8,64,128]{2,1,0:T(8,128)(2,1)} %copy.40), calls=%async_computation.3 | async-start | bytes 262144 | tf_op jit(solution)/shard_map/all_to_all | solution.py:80
  79.6 10.7 %all-to-all-start.2 = ((bf16[8,64,128]{2,1,0:T(8,128)(2,1)}), bf16[8,64,128]{2,1,0:T(8,128)(2,1)S(1)}, u32[]{:S(2)}, u32[]{:S(2)}) async-start(bf16[8,64,128]{2,1,0:T(8,128)(2,1)} %copy.35), calls=%async_computation.2 | async-start | bytes 262144 | tf_op jit(solution)/shard_map/all_to_all | solution.py:73
  93.7 42.0 %copy-start.3 = (bf16[64,1024]{1,0:T(8,128)(2,1)}, bf16[64,1024]{1,0:T(8,128)(2,1)S(1)}, u32[]{:S(2)}) copy-start(bf16[64,1024]{1,0:T(8,128)(2,1)S(1)} %convolution_convert_fusion) | copy-start | bytes 393220
Sparse Core Ops, SparseCore 0:
  9.5 25.5 all-gather.2
where the time goes:
time: 143 us
  blocking collectives  62.9 us (44%)
  waiting for transfers between devices  25.7 us (18%)
  matrix products  15.6 us (11%)
  starting transfers between devices  15.1 us (11%)
  between operations  14.4 us (10%)
  local copies, waits for them, and re-layouts  7.77 us (5%)
    psum x1, blocking collectives, per_device(): summed = lax.psum(ordered, 'tiles')  33.9 us
    all_gather x1, blocking collectives, per_device(): all_rows = lax.all_gather(tile_rows, 'tiles', axis=0, tiled=True)  22.5 us
    all_to_all x2, waiting for transfers between devices, per_device(): lax.all_to_all(send_lower, 'tiles', split_axis=0, concat_axis=0, tiled=True)  12.7 us
    all_to_all x2, waiting for transfers between devices, per_device(): lax.all_to_all(send_upper, 'tiles', split_axis=0, concat_axis=0, tiled=True)  12.2 us
    dot_general x3, matrix products, precondition(): jnp.dot(resid, whole_inverse, preferred_element_type=jnp.float32)  8.6 us
    all_to_all x2, starting transfers between devices, per_device(): lax.all_to_all(send_upper, 'tiles', split_axis=0, concat_axis=0, tiled=True)  8.37 us
    all_to_all x2, starting transfers between devices, per_device(): lax.all_to_all(send_lower, 'tiles', split_axis=0, concat_axis=0, tiled=True)  6.74 us
    all_gather x1, blocking collectives, per_device(): lax.all_gather(iterate, 'rhs', axis=0, tiled=True)  6.5 us
  transfers between devices with their start and end apart: 5, of which 4 were waited for; matrix products, arithmetic and copies ran while one was open for 6% of the time, Pallas kernels for 0%

commit v1 on v0

--- a/solution.py
+++ b/solution.py
@@ -1,8 +1,11 @@
+import functools
 import math
 
 import jax
 import jax.numpy as jnp
 from jax import lax
+from jax.experimental import pallas as pl
+from jax.experimental.pallas import tpu as pltpu
 from jax.sharding import PartitionSpec as P
 
 ITERS = 2
@@ -17,7 +20,7 @@
     return (jnp.exp(-2.0 * dist_sq) * amplitude).astype(jnp.bfloat16)
 
 
-def per_device(
+def sparse_device(
     rhs_rows,
     diag_inverse,
     u_factors,
@@ -55,7 +58,7 @@
         )
 
     iterate = precondition(rhs_rows)
-    for sweep in range(ITERS):
+    for _ in range(ITERS):
         lower = jnp.einsum("cb,kbr->kcr", iterate, v_slots, preferred_element_type=jnp.float32)
         lower = (lower * rank_mask[:, None, :]).astype(jnp.bfloat16)
         upper = jnp.einsum(
@@ -105,6 +108,361 @@
     return (iterate, owned_sums)
 
 
+CONTRACT_LAST = (((1,), (1,)), ((), ()))
+
+
+def xor_pairs(size, bit):
+    return [(here, here ^ bit) for here in range(size)]
+
+
+def from_shard(piece, axis, size, bit):
+    return lax.ppermute(piece, axis, xor_pairs(size, bit))
+
+
+def peer_at(tile_here, shift, tiles_count):
+    there = tile_here + shift
+    return jnp.where(there >= tiles_count, there - tiles_count, there)
+
+
+def start_copies(sources, targets, sems):
+    copies = [
+        pltpu.make_async_copy(source, target, sems.at[n])
+        for n, (source, target) in enumerate(zip(sources, targets, strict=True))
+    ]
+    for copy in copies:
+        copy.start()
+    return copies
+
+
+def wait_for(copies):
+    for copy in copies:
+        copy.wait()
+
+
+def in_hbm(array):
+    return pltpu.with_memory_space_constraint(array, pltpu.HBM)
+
+
+def pack_kernel(cand_hbm, owner_hbm, rows_hbm, packed_ref, cand_ref, owner_ref, rows_ref, sems):
+    sources, targets = (cand_hbm, owner_hbm, rows_hbm), (cand_ref, owner_ref, rows_ref)
+    wait_for(start_copies(sources, targets, sems))
+    parts = [cand_ref[dim : dim + 1, :] for dim in range(cand_ref.shape[0])]
+    parts += [owner_ref[...].astype(jnp.float32), rows_ref[...].astype(jnp.float32)]
+    length = sum(part.shape[1] for part in parts)
+    parts.append(jnp.zeros((1, packed_ref.shape[2] - length), jnp.float32))
+    packed = jnp.concatenate(parts, axis=1)
+    packed_ref[...] = jnp.broadcast_to(packed[None], packed_ref.shape)
+
+
+def plan_into(plan_ref, rows_ref, ranks_ref, lane):
+    slot_count = ranks_ref.shape[1]
+    tiles_count = plan_ref.shape[1]
+    tile_here = lax.axis_index("tiles")
+    for shift in range(tiles_count):
+        there = peer_at(tile_here, shift, tiles_count)
+        out_slot = jnp.int32(0)
+        in_slot = jnp.int32(0)
+        for slot in range(1, slot_count):
+            listed_here = rows_ref[tile_here, 0, lane + slot].astype(jnp.int32)
+            listed_there = rows_ref[there, 0, lane + slot].astype(jnp.int32)
+            out_slot = jnp.where(listed_here == there, slot, out_slot)
+            in_slot = jnp.where(listed_there == tile_here, slot, in_slot)
+        plan_ref[0, shift] = there
+        plan_ref[1, shift] = out_slot
+        plan_ref[2, shift] = in_slot
+        plan_ref[3, shift] = ranks_ref[0, out_slot]
+        plan_ref[4, shift] = lax.axis_index("rhs")
+
+
+def prepare_kernel(
+    packed_ref, ranks_hbm, points_hbm, *refs, amplitude, group_len, kept_count
+):
+    kept_hbm, refs = refs[:kept_count], refs[kept_count:]
+    plan_ref, cross_ref, *refs = refs
+    kept_refs, (ranks_ref, points_ref, rows_ref, kept_sems, small_sems) = (
+        refs[:kept_count],
+        refs[kept_count:],
+    )
+    tiles_count = plan_ref.shape[1]
+    rhs_count = packed_ref.shape[0] // tiles_count
+    dims = points_ref.shape[0]
+    total = rhs_count * group_len
+    first_lane = (dims + 1) * group_len // 128 * 128
+    told = [packed_ref.at[tile * rhs_count, :, first_lane:] for tile in range(tiles_count)]
+    smalls = start_copies(
+        [points_hbm, ranks_hbm, *told],
+        [points_ref, ranks_ref, *(rows_ref.at[tile] for tile in range(tiles_count))],
+        small_sems,
+    )
+    copies = start_copies(kept_hbm, kept_refs, kept_sems)
+
+    def joined(index):
+        lanes = slice(index * group_len, (index + 1) * group_len)
+        return jnp.concatenate([packed_ref[group, :, lanes] for group in range(rhs_count)], axis=1)
+
+    columns = jnp.concatenate([joined(dim) for dim in range(dims)], axis=0).T
+    smalls[0].wait()
+    dist_sq = None
+    for dim in range(dims):
+        gap = columns[:, dim : dim + 1] - points_ref[dim : dim + 1, :]
+        dist_sq = gap * gap if dist_sq is None else dist_sq + gap * gap
+    cross = (jnp.exp(-2.0 * dist_sq) * amplitude).astype(jnp.bfloat16)
+    owner = joined(dims).astype(jnp.int32)
+    hot = lax.broadcasted_iota(jnp.int32, (tiles_count, total), 0) == owner
+    before = lax.broadcasted_iota(jnp.int32, (total, total), 0)
+    after = lax.broadcasted_iota(jnp.int32, (total, total), 1)
+    earlier = (before < after) & (before // group_len == after // group_len)
+    counts = jnp.dot(
+        hot.astype(jnp.float32).astype(jnp.bfloat16),
+        earlier.astype(jnp.float32).astype(jnp.bfloat16),
+        preferred_element_type=jnp.float32,
+    )
+    within = jnp.sum(jnp.where(hot, counts, 0.0), axis=0, keepdims=True).astype(jnp.int32)
+    piece = lax.broadcasted_iota(jnp.int32, (1, total), 1) // group_len
+    place = (within * tiles_count + owner) * rhs_count + piece
+    order = (before == place).astype(jnp.float32).astype(jnp.bfloat16)
+    ordered = jnp.dot(order, cross, preferred_element_type=jnp.float32)
+    cross_ref[...] = ordered.astype(jnp.bfloat16)
+    wait_for(smalls[1:])
+    plan_into(plan_ref, rows_ref, ranks_ref, (dims + 1) * group_len - first_lane)
+    wait_for(copies)
+
+
+def pair_at(plan_ref, u_ref, v_ref, shift):
+    return jnp.concatenate([v_ref[plan_ref[1, shift]], u_ref[plan_ref[2, shift]]], axis=1)
+
+
+def rank_mask(plan_ref, shift, width):
+    lanes = lax.broadcasted_iota(jnp.int32, (1, width), 1)
+    return lanes < plan_ref[3, shift]
+
+
+def store_products(iterate, u_ref, v_ref, send_ref, plan_ref):
+    width = u_ref.shape[2]
+    for shift in range(1, plan_ref.shape[1]):
+        product = jnp.dot(
+            iterate, pair_at(plan_ref, u_ref, v_ref, shift), preferred_element_type=jnp.float32
+        )
+        there = plan_ref[0, shift]
+        lower = jnp.where(rank_mask(plan_ref, shift, width), product[:, :width], 0.0)
+        send_ref[there, :, :width] = lower.astype(jnp.bfloat16)
+        send_ref[there, :, width:] = product[:, width:].astype(jnp.bfloat16)
+    send_ref[plan_ref[0, 0]] = jnp.zeros(send_ref.shape[1:], jnp.bfloat16)
+
+
+def precondition_into(resid, inverse_refs, column_here, out_ref):
+    for d, inverse_ref in enumerate(inverse_refs):
+        columns = inverse_ref.shape[1]
+        start = pl.multiple_of((column_here ^ d) * columns, columns)
+        out_ref[:, pl.ds(start, columns)] = jnp.dot(
+            resid, inverse_ref[...], preferred_element_type=jnp.float32
+        ).astype(jnp.bfloat16)
+
+
+def residual_into(rhs_ref, recv_ref, u_ref, v_ref, plan_ref, total_ref, resid_ref):
+    width = u_ref.shape[2]
+    for shift in range(1, plan_ref.shape[1]):
+        got = recv_ref[plan_ref[0, shift]]
+        upper = jnp.where(rank_mask(plan_ref, shift, width), got[:, width:], jnp.bfloat16(0))
+        term = lax.dot_general(
+            jnp.concatenate([upper, got[:, :width]], axis=1),
+            pair_at(plan_ref, u_ref, v_ref, shift),
+            CONTRACT_LAST,
+            preferred_element_type=jnp.float32,
+        )
+        if shift == 1:
+            total_ref[...] = term
+        else:
+            total_ref[...] += term
+    resid_ref[...] = (rhs_ref[...].astype(jnp.float32) - total_ref[...]).astype(jnp.bfloat16)
+
+
+def first_kernel(plan_ref, rhs_ref, u_ref, v_ref, *refs):
+    inverse_refs, (send_ref, iterate_ref) = refs[:-2], refs[-2:]
+    precondition_into(rhs_ref[...], inverse_refs, plan_ref[4, 0], iterate_ref)
+    store_products(iterate_ref[...], u_ref, v_ref, send_ref, plan_ref)
+
+
+def middle_kernel(plan_ref, recv_ref, rhs_ref, u_ref, v_ref, *refs):
+    inverse_refs, (send_ref, iterate_ref, total_ref, resid_ref) = refs[:-4], refs[-4:]
+    residual_into(rhs_ref, recv_ref, u_ref, v_ref, plan_ref, total_ref, resid_ref)
+    precondition_into(resid_ref[...], inverse_refs, plan_ref[4, 0], iterate_ref)
+    store_products(iterate_ref[...], u_ref, v_ref, send_ref, plan_ref)
+
+
+def last_kernel(plan_ref, recv_ref, rhs_ref, u_ref, v_ref, cross_ref, *refs):
+    inverse_refs, (iterate_ref, partial_ref, total_ref, resid_ref) = refs[:-4], refs[-4:]
+    residual_into(rhs_ref, recv_ref, u_ref, v_ref, plan_ref, total_ref, resid_ref)
+    precondition_into(resid_ref[...], inverse_refs, plan_ref[4, 0], iterate_ref)
+    values = lax.dot_general(
+        cross_ref[...], iterate_ref[...], CONTRACT_LAST, preferred_element_type=jnp.float32
+    )
+    devices, columns = partial_ref.shape[0], values.shape[1]
+    for place in range(values.shape[0] // devices):
+        partial_ref[:, 0, place * columns : (place + 1) * columns] = values[
+            place * devices : (place + 1) * devices, :
+        ]
+
+
+def sum_kernel(parts_ref, out_ref, *, rhs_count):
+    owned = out_ref.shape[0]
+    columns = parts_ref.shape[2] // owned
+    for group in range(rhs_count):
+        total = parts_ref[group]
+        for part in range(group + rhs_count, parts_ref.shape[0], rhs_count):
+            total += parts_ref[part]
+        for place in range(owned):
+            out_ref[place : place + 1, group * columns : (group + 1) * columns] = total[
+                :, place * columns : (place + 1) * columns
+            ]
+
+
+SMEM = pl.BlockSpec(memory_space=pltpu.SMEM)
+VMEM = pl.BlockSpec(memory_space=pltpu.VMEM)
+HBM = pl.BlockSpec(memory_space=pltpu.HBM)
+PARAMS = pltpu.CompilerParams(vmem_limit_bytes=16 << 20)
+
+
+def dense_device(
+    rhs_rows,
+    diag_inverse,
+    u_factors,
+    v_factors,
+    tile_rows,
+    tile_ranks,
+    point_coords,
+    cand_coords,
+    owner,
+):
+    tiles_count = lax.axis_size("tiles")
+    rhs_count = lax.axis_size("rhs")
+    rows_here, block_len = rhs_rows.shape
+    slot_count, width = u_factors.shape[1], u_factors.shape[3]
+
+    inverse = {0: diag_inverse}
+    bit = rhs_count // 2
+    while bit > 1:
+        for d, piece in list(inverse.items()):
+            inverse[d ^ bit] = from_shard(piece, "rhs", rhs_count, bit)
+        bit //= 2
+    inverse[1] = from_shard(diag_inverse, "rhs", rhs_count, 1)
+    devices = tiles_count * rhs_count
+    dims, group_len = cand_coords.shape
+    total = rhs_count * group_len
+    lanes = -(-((dims + 1) * group_len + slot_count) // 128) * 128
+    packed = pl.pallas_call(
+        pack_kernel,
+        out_shape=jax.ShapeDtypeStruct((devices, 1, lanes), jnp.float32),
+        in_specs=[HBM] * 3,
+        out_specs=VMEM,
+        compiler_params=PARAMS,
+        scratch_shapes=[
+            pltpu.VMEM(cand_coords.shape, jnp.float32),
+            pltpu.VMEM((1, group_len), jnp.int32),
+            pltpu.VMEM(tile_rows.shape, jnp.int32),
+            pltpu.SemaphoreType.DMA((3,)),
+        ],
+    )(in_hbm(cand_coords), in_hbm(owner[None, :]), in_hbm(tile_rows))
+    told = lax.all_to_all(packed, ("tiles", "rhs"), 0, 0, tiled=True)
+    amplitude = 4.0 / math.sqrt(block_len * tiles_count)
+    pieces_far = [d for d in inverse if d > 1]
+    held, told = lax.optimization_barrier(([inverse[d] for d in pieces_far], told))
+    for d, piece in zip(pieces_far, held, strict=True):
+        inverse[d] = piece
+        inverse[d ^ 1] = from_shard(piece, "rhs", rhs_count, 1)
+    loaded = (rhs_rows, u_factors[0], v_factors[0], diag_inverse)
+    table_lanes = lanes - (dims + 1) * group_len // 128 * 128
+    plan, cross, *kept, own_piece = pl.pallas_call(
+        functools.partial(
+            prepare_kernel, amplitude=amplitude, group_len=group_len, kept_count=len(loaded)
+        ),
+        out_shape=(
+            jax.ShapeDtypeStruct((5, tiles_count), jnp.int32),
+            jax.ShapeDtypeStruct((total, block_len), jnp.bfloat16),
+            *(pltpu.VMEM(array.shape, array.dtype) for array in loaded),
+        ),
+        in_specs=[VMEM] + [HBM] * (2 + len(loaded)),
+        out_specs=(SMEM, *[VMEM] * (1 + len(loaded))),
+        compiler_params=PARAMS,
+        scratch_shapes=[
+            pltpu.SMEM(tile_ranks.shape, jnp.int32),
+            pltpu.VMEM(point_coords.shape, jnp.float32),
+            pltpu.SMEM((tiles_count, 1, table_lanes), jnp.float32),
+            pltpu.SemaphoreType.DMA((len(loaded),)),
+            pltpu.SemaphoreType.DMA((2 + tiles_count,)),
+        ],
+    )(told, *(in_hbm(array) for array in (tile_ranks, point_coords, *loaded)))
+
+    def resident(arrays):
+        return [pltpu.with_memory_space_constraint(array, pltpu.VMEM) for array in arrays]
+
+    def weights():
+        return resident(kept), resident([own_piece, *(inverse[d] for d in range(1, rhs_count))])
+
+    sent = jax.ShapeDtypeStruct((tiles_count, rows_here, 2 * width), jnp.bfloat16)
+    rounded = jax.ShapeDtypeStruct((rows_here, block_len), jnp.bfloat16)
+    block = pltpu.VMEM(rounded.shape, jnp.bfloat16)
+    wide = pltpu.VMEM(rounded.shape, jnp.float32)
+
+    def exchange(send):
+        return lax.all_to_all(send, "tiles", 0, 0, tiled=True)
+
+    kept, pieces = weights()
+    send = pl.pallas_call(
+        first_kernel,
+        out_shape=sent,
+        in_specs=[SMEM] + [VMEM] * (3 + rhs_count),
+        out_specs=VMEM,
+        compiler_params=PARAMS,
+        scratch_shapes=[block],
+    )(plan, *kept, *pieces)
+    for _ in range(ITERS - 1):
+        recv = exchange(send)
+        kept, pieces = weights()
+        send = pl.pallas_call(
+            middle_kernel,
+            out_shape=sent,
+            in_specs=[SMEM] + [VMEM] * (4 + rhs_count),
+            out_specs=VMEM,
+            compiler_params=PARAMS,
+            scratch_shapes=[block, wide, block],
+        )(plan, recv, *kept, *pieces)
+    recv = exchange(send)
+    owned = total // devices
+    kept, pieces = weights()
+    iterate, partial_values = pl.pallas_call(
+        last_kernel,
+        out_shape=(
+            rounded,
+            jax.ShapeDtypeStruct((devices, 1, owned * rows_here), jnp.float32),
+        ),
+        in_specs=[SMEM] + [VMEM] * (5 + rhs_count),
+        out_specs=(VMEM, VMEM),
+        compiler_params=PARAMS,
+        scratch_shapes=[wide, block],
+    )(plan, recv, *kept, cross, *pieces)
+    parts = lax.all_to_all(partial_values, ("tiles", "rhs"), 0, 0, tiled=True)
+    owned_sums = pl.pallas_call(
+        functools.partial(sum_kernel, rhs_count=rhs_count),
+        out_shape=jax.ShapeDtypeStruct((owned, rows_here * rhs_count), jnp.float32),
+        in_specs=[VMEM],
+        out_specs=VMEM,
+        compiler_params=PARAMS,
+    )(parts)
+    return (iterate, owned_sums)
+
+
+def takes_dense(slot_count, tiles_count, rhs_count):
+    return slot_count == tiles_count - 1 and rhs_count > 1 and rhs_count & (rhs_count - 1) == 0
+
+
+def per_device(rhs_rows, diag_inverse, u_factors, *others):
+    tiles_count, rhs_count = lax.axis_size("tiles"), lax.axis_size("rhs")
+    dense = takes_dense(u_factors.shape[1], tiles_count, rhs_count)
+    body = dense_device if dense else sparse_device
+    return body(rhs_rows, diag_inverse, u_factors, *others)
+
+
 def solution(mesh):
     in_specs = (
         P("rhs", "tiles"),

time: 143 us -> 66.6 us (0.47)
  blocking collectives: 62.9 us -> 37.3 us
  waiting for transfers between devices: 25.7 us -> 7.19 us
  matrix products: 15.6 us -> 0 us
  between operations: 14.4 us -> 0.69 us
  Pallas kernels: 0 us -> 12.9 us
  local copies, waits for them, and re-layouts: 7.77 us -> 0 us
  starting transfers between devices: 15.1 us -> 8.28 us
    all_to_all x0 -> x3, blocking collectives: none -> 37.3 us  [the longest x2 26.7 us: exchange(): return lax.all_to_all(send, 'tiles', 0, 0, tiled=True)]
    psum x1 -> x0, blocking collectives: 33.9 us -> none  [per_device(): summed = lax.psum(ordered, 'tiles')]
    all_gather x2 -> x0, blocking collectives: 29 us -> none  [the longest x1 22.5 us: per_device(): all_rows = lax.all_gather(tile_rows, 'tiles', axis=0, tiled=True)]
    all_to_all x4 -> x1, waiting for transfers between devices: 25 us -> 7.18 us  [dense_device(): told = lax.all_to_all(packed, ('tiles', 'rhs'), 0, 0, tiled=True)]
    dot_general x19 -> x0, matrix products: 15.6 us -> none  [the longest x3 8.6 us: precondition(): jnp.dot(resid, whole_inverse, preferred_element_type=jnp.float32)]
    pallas_call x0 -> x6, Pallas kernels: none -> 12.9 us  [the longest x1 3.02 us: dense_device(): pl.pallas_call(functools.partial(prepare_kernel, amplitude=amplitude, gro...]
    all_to_all x4 -> x1, starting transfers between devices: 15.1 us -> 4.93 us  [dense_device(): told = lax.all_to_all(packed, ('tiles', 'rhs'), 0, 0, tiled=True)]
    scatter x2 -> x0, local copies, waits for them, and re-layouts: 4.2 us -> none  [the longest x1 3.45 us: per_device(): jnp.zeros(all_rows.shape, jnp.int32).at[all_rows, slot_range[None, :]]]
  transfers between devices with their start and end apart: 5 -> 4, of which waited for: 4 -> 1; matrix products, arithmetic and copies ran while one was open for 6% -> 0% of each run, Pallas kernels for 0% -> 7%
where the time goes in v1:
time: 66.6 us; the launch traced here: 66.3 us
  blocking collectives  37.3 us (56%)
  Pallas kernels  12.9 us (19%)
  starting transfers between devices  8.28 us (12%)
  waiting for transfers between devices  7.19 us (11%)
  between operations  0.69 us (1%)
    all_to_all x2, blocking collectives, exchange(): return lax.all_to_all(send, 'tiles', 0, 0, tiled=True)  26.7 us
    all_to_all x1, blocking collectives, dense_device(): parts = lax.all_to_all(partial_values, ('tiles', 'rhs'), 0, 0, tiled=True)  10.6 us
    all_to_all x1, waiting for transfers between devices, dense_device(): told = lax.all_to_all(packed, ('tiles', 'rhs'), 0, 0, tiled=True)  7.18 us
    all_to_all x1, starting transfers between devices, dense_device(): told = lax.all_to_all(packed, ('tiles', 'rhs'), 0, 0, tiled=True)  4.93 us
    ppermute x3, starting transfers between devices, from_shard(): return lax.ppermute(piece, axis, xor_pairs(size, bit))  3.35 us
    pallas_call x1, Pallas kernels, dense_device(): pl.pallas_call(functools.partial(prepare_kernel, amplitude=amplitude, gro...  3.02 us
    pallas_call x1, Pallas kernels, dense_device(): pl.pallas_call(middle_kernel, out_shape=sent, in_specs=[SMEM] + [VMEM] *...  2.97 us
    pallas_call x1, Pallas kernels, dense_device(): pl.pallas_call(last_kernel, out_shape=(rounded, jax.ShapeDtypeStruct((dev...  2.84 us
  transfers between devices with their start and end apart: 4, of which 1 were waited for; matrix products, arithmetic and copies ran while one was open for 0% of the time, Pallas kernels for 7%

profile of v1, /device:TPU:0, one launch (start us, length us, event | category | flops | bytes accessed | tf_op | source)
XLA Modules:
  0.0 66.3 jit_solution(10892108780076276479)
XLA Ops:
  0.6 3.0 %collective-permute-start = (bf16[1024,256]{1,0:T(8,128)(2,1)}, bf16[1024,256]{1,0:T(8,128)(2,1)S(1)}, u32[]{:S(2)}, u32[]{:S(2)}) collective-permute-start(bf16[1024,256]{1,0:T(8,128)(2,1)} %refs_3_.1), channel_id=1, source_target_pairs={{0,2},{1,3},{2,0},{3,1},{4,6},{5,7},{6,4},{7,5},{8,10},{9,11},{10,... | collective-permute-start | bytes 1572872 | tf_op jit(solution)/shard_map/ppermute | solution.py:119
  3.7 1.4 %shard_map.104 = f32[32,1,384]{2,1,0:T(1,128)} custom-call(f32[8,32]{1,0:T(8,128)} %cand_hbm.1, s32[1,32]{1,0:T(1,128)} %bitcast.5, s32[1,7]{1,0:T(1,128)} %rows_hbm.1), custom_call_target="tpu_custom_call" | custom-call | tf_op jit(solution)/shard_map/pallas_call | solution.py:353
  5.1 4.9 %all-to-all-start = ((f32[32,1,384]{2,1,0:T(1,128)}), f32[32,1,384]{2,1,0:T(1,128)S(1)}, u32[]{:S(2)}, u32[]{:S(2)}) async-start(f32[32,1,384]{2,1,0:T(1,128)} %shard_map.104), calls=%async_computation | async-start | bytes 98304 | tf_op jit(solution)/shard_map/all_to_all | solution.py:366
  10.0 0.3 collective-permute-start.1
  10.3 7.2 %all-to-all-done.packed_ref = f32[32,1,384]{2,1,0:T(1,128)S(1)} async-done(((f32[32,1,384]{2,1,0:T(1,128)}), f32[32,1,384]{2,1,0:T(1,128)S(1)}, u32[]{:S(2)}, u32[]{:S(2)}) %all-to-all-start) | async-done | bytes 49184 | tf_op jit(solution)/shard_map/all_to_all | solution.py:366
  17.5 0.0 collective-permute-done.refs_2_
  17.5 0.0 collective-permute-start.2
  17.5 3.0 %shard_map.105 = (s32[5,8]{1,0:T(8,128)S(1)}, bf16[128,1024]{1,0:T(8,128)(2,1)S(1)}, bf16[64,1024]{1,0:T(8,128)(2,1)S(1)}, bf16[7,1024,128]{2,1,0:T(8,128)(2,1)S...) custom-call(f32[32,1,384]{2,1,0:T(1,128)S(1)} %all-to-all-done.packed_ref, s32[1,7]{1,0:T(1,128)} %ranks_hbm.1, ...), custom_call_target="tpu_custom_call" | custom-call | tf_op jit(solution)/shard_map/pallas_call | solution.py:375
  20.6 0.0 collective-permute-done.1.refs_1_
  20.6 0.0 collective-permute-done.2.refs_3_
  20.6 1.9 %shard_map.106 = bf16[8,64,256]{2,1,0:T(8,128)(2,1)S(1)} custom-call(s32[5,8]{1,0:T(8,128)S(1)} %get-tuple-element.13.plan_ref, bf16[64,1024]{1,0:T(8,128)(2,1)S(1)} %get-tuple-element.14.rhs_ref, bf16[7,1024,128]{2,1,0:T(8,128)(2,1)S(1)} %get-tuple-element.15.u_ref, bf16[7,1024,128]{2,1,0:T(8,128)(2,1)S(1)} %get-tuple-element.16.v_ref, ...), custom_call_target="tpu_custom_call" | custom-call | tf_op jit(solution)/shard_map/pallas_call | solution.py:411
  22.5 14.3 %all_to_all.20.recv_ref = bf16[8,64,256]{2,1,0:T(8,128)(2,1)S(1)} all-to-all(bf16[8,64,256]{2,1,0:T(8,128)(2,1)S(1)} %shard_map.106), channel_id=1, replica_groups=mesh['tiles'=8,'rhs'=4] {'tiles'}, dimensions={0} | all-to-all | bytes 524288 | tf_op jit(solution)/shard_map/all_to_all | solution.py:408
  36.8 3.0 %shard_map.107 = bf16[8,64,256]{2,1,0:T(8,128)(2,1)S(1)} custom-call(s32[5,8]{1,0:T(8,128)S(1)} %get-tuple-element.13.plan_ref, bf16[8,64,256]{2,1,0:T(8,128)(2,1)S(1)} %all_to_all.20.recv_ref, bf16[64,1024]{1,0:T(8,128)(2,1)S(1)} %get-tuple-element.14.rhs_ref, bf16[7,1024,128]{2,1,0:T(8,128)(2,1)S(1)} %get-tuple-element.15.u_ref, ...), custom_call_target="tpu_custom_call" | custom-call | tf_op jit(solution)/shard_map/pallas_call | solution.py:422
  39.8 12.5 %all_to_all.21.recv_ref = bf16[8,64,256]{2,1,0:T(8,128)(2,1)S(1)} all-to-all(bf16[8,64,256]{2,1,0:T(8,128)(2,1)S(1)} %shard_map.107), channel_id=1, replica_groups=mesh['tiles'=8,'rhs'=4] {'tiles'}, dimensions={0} | all-to-all | bytes 524288 | tf_op jit(solution)/shard_map/all_to_all | solution.py:408
  52.2 2.8 %shard_map.108 = (bf16[64,1024]{1,0:T(8,128)(2,1)}, f32[32,1,256]{2,1,0:T(1,128)S(1)}) custom-call(s32[5,8]{1,0:T(8,128)S(1)} %get-tuple-element.13.plan_ref, bf16[8,64,256]{2,1,0:T(8,128)(2,1)S(1)} %all_to_all.21.recv_ref, bf16[64,1024]{1,0:T(8,128)(2,1)S(1)} %get-tuple-element.14.rhs_ref, bf16[7,1024,128]{2,1,0:T(8,128)(2,1)S(1)} %get-tuple-element.15.u_ref, ...), custom_call_target="tpu_custom_call" | custom-call | tf_op jit(solution)/shard_map/pallas_call | solution.py:433
  55.1 10.6 %all_to_all.22.parts_ref = f32[32,1,256]{2,1,0:T(1,128)S(1)} all-to-all(f32[32,1,256]{2,1,0:T(1,128)S(1)} %get-tuple-element.21), channel_id=1, replica_groups=mesh['tiles'=8,'rhs'=4] {'tiles','rhs'}, dimensions={0} | all-to-all | bytes 65536 | tf_op jit(solution)/shard_map/all_to_all | solution.py:444
  65.7 0.7 %shard_map.109 = f32[4,256]{1,0:T(4,128)} custom-call(f32[32,1,256]{2,1,0:T(1,128)S(1)} %all_to_all.22.parts_ref), custom_call_target="tpu_custom_call" | custom-call | tf_op jit(solution)/shard_map/pallas_call | solution.py:445
Async XLA Ops:
  0.6 16.9 %collective-permute-start = (bf16[1024,256]{1,0:T(8,128)(2,1)}, bf16[1024,256]{1,0:T(8,128)(2,1)S(1)}, u32[]{:S(2)}, u32[]{:S(2)}) collective-permute-start(bf16[1024,256]{1,0:T(8,128)(2,1)} %refs_3_.1), channel_id=1, source_target_pairs={{0,2},{1,3},{2,0},{3,1},{4,6},{5,7},{6,4},{7,5},{8,10},{9,11},{10,... | collective-permute-start | bytes 1572872 | tf_op jit(solution)/shard_map/ppermute | solution.py:119
  5.1 12.4 %all-to-all-start = ((f32[32,1,384]{2,1,0:T(1,128)}), f32[32,1,384]{2,1,0:T(1,128)S(1)}, u32[]{:S(2)}, u32[]{:S(2)}) async-start(f32[32,1,384]{2,1,0:T(1,128)} %shard_map.104), calls=%async_computation | async-start | bytes 98304 | tf_op jit(solution)/shard_map/all_to_all | solution.py:366
  10.0 10.5 %collective-permute-start.1 = (bf16[1024,256]{1,0:T(8,128)(2,1)}, bf16[1024,256]{1,0:T(8,128)(2,1)S(1)}, u32[]{:S(2)}, u32[]{:S(2)}) collective-permute-start(bf16[1024,256]{1,0:T(8,128)(2,1)} %refs_3_.1), channel_id=1, source_target_pairs={{0,1},{1,0},{2,3},{3,2},{4,5},{5,4},{6,7},{7,6},{8,9},{9,8},{10,11... | collective-permute-start | bytes 1572872 | tf_op jit(solution)/shard_map/ppermute | solution.py:119
  17.5 3.0 %collective-permute-start.2 = (bf16[1024,256]{1,0:T(8,128)(2,1)S(1)}, bf16[1024,256]{1,0:T(8,128)(2,1)S(1)}, u32[]{:S(2)}, u32[]{:S(2)}) collective-permute-start(bf16[1024,256]{1,0:T(8,128)(2,1)S(1)} %collective-permute-done.refs_2_), channel_id=1, source_target_pairs={{0,1},{1,0},{2,3},{3,2},{4,5},{5,4},{6,7},{7,6},{8,9},{9,8},{10,11... | collective-permute-start | bytes 1572872 | tf_op jit(solution)/shard_map/ppermute | solution.py:119

commit v2 on v1

--- a/solution.py
+++ b/solution.py
@@ -143,71 +143,59 @@
     return pltpu.with_memory_space_constraint(array, pltpu.HBM)
 
 
-def pack_kernel(cand_hbm, owner_hbm, rows_hbm, packed_ref, cand_ref, owner_ref, rows_ref, sems):
-    sources, targets = (cand_hbm, owner_hbm, rows_hbm), (cand_ref, owner_ref, rows_ref)
+def load_kernel(*refs):
+    count = len(refs) // 2
+    wait_for(start_copies(refs[:count], refs[count : 2 * count], refs[-1]))
+
+
+def pack_kernel(
+    cand_hbm, owner_hbm, rows_hbm, listed_ref, cand_ref, coords_ref, owner_ref, rows_ref, sems
+):
+    sources, targets = (cand_hbm, owner_hbm, rows_hbm), (coords_ref, owner_ref, rows_ref)
     wait_for(start_copies(sources, targets, sems))
-    parts = [cand_ref[dim : dim + 1, :] for dim in range(cand_ref.shape[0])]
-    parts += [owner_ref[...].astype(jnp.float32), rows_ref[...].astype(jnp.float32)]
-    length = sum(part.shape[1] for part in parts)
-    parts.append(jnp.zeros((1, packed_ref.shape[2] - length), jnp.float32))
-    packed = jnp.concatenate(parts, axis=1)
-    packed_ref[...] = jnp.broadcast_to(packed[None], packed_ref.shape)
-
-
-def plan_into(plan_ref, rows_ref, ranks_ref, lane):
+    dims, slot_count = coords_ref.shape[0], rows_ref.shape[1]
+    cand_ref[:dims, :] = coords_ref[...]
+    cand_ref[dims:, :] = owner_ref[...].astype(jnp.float32)
+    listed_ref[:, :, :slot_count] = jnp.broadcast_to(
+        rows_ref[...][None], (*listed_ref.shape[:2], slot_count)
+    )
+    listed_ref[:, :, slot_count:] = jnp.zeros(
+        (*listed_ref.shape[:2], listed_ref.shape[2] - slot_count), jnp.int32
+    )
+
+
+def plan_kernel(
+    listed_in, ranks_hbm, u_hbm, own_hbm, plan_ref, u_ref, own_ref, listed_ref, ranks_ref, sems
+):
+    copies = start_copies(
+        (listed_in, ranks_hbm, u_hbm, own_hbm), (listed_ref, ranks_ref, u_ref, own_ref), sems
+    )
     slot_count = ranks_ref.shape[1]
     tiles_count = plan_ref.shape[1]
     tile_here = lax.axis_index("tiles")
+    wait_for(copies[:2])
     for shift in range(tiles_count):
         there = peer_at(tile_here, shift, tiles_count)
         out_slot = jnp.int32(0)
         in_slot = jnp.int32(0)
         for slot in range(1, slot_count):
-            listed_here = rows_ref[tile_here, 0, lane + slot].astype(jnp.int32)
-            listed_there = rows_ref[there, 0, lane + slot].astype(jnp.int32)
-            out_slot = jnp.where(listed_here == there, slot, out_slot)
-            in_slot = jnp.where(listed_there == tile_here, slot, in_slot)
+            out_slot = jnp.where(listed_ref[tile_here, 0, slot] == there, slot, out_slot)
+            in_slot = jnp.where(listed_ref[there, 0, slot] == tile_here, slot, in_slot)
         plan_ref[0, shift] = there
         plan_ref[1, shift] = out_slot
         plan_ref[2, shift] = in_slot
         plan_ref[3, shift] = ranks_ref[0, out_slot]
         plan_ref[4, shift] = lax.axis_index("rhs")
-
-
-def prepare_kernel(
-    packed_ref, ranks_hbm, points_hbm, *refs, amplitude, group_len, kept_count
-):
-    kept_hbm, refs = refs[:kept_count], refs[kept_count:]
-    plan_ref, cross_ref, *refs = refs
-    kept_refs, (ranks_ref, points_ref, rows_ref, kept_sems, small_sems) = (
-        refs[:kept_count],
-        refs[kept_count:],
-    )
-    tiles_count = plan_ref.shape[1]
-    rhs_count = packed_ref.shape[0] // tiles_count
-    dims = points_ref.shape[0]
+    wait_for(copies[2:])
+
+
+def cross_kernel(points_ref, *refs, amplitude, tiles_count):
+    cand_refs, cross_ref = refs[:-1], refs[-1]
+    rhs_count = len(cand_refs)
+    dims, group_len = points_ref.shape[0], cand_refs[0].shape[1]
     total = rhs_count * group_len
-    first_lane = (dims + 1) * group_len // 128 * 128
-    told = [packed_ref.at[tile * rhs_count, :, first_lane:] for tile in range(tiles_count)]
-    smalls = start_copies(
-        [points_hbm, ranks_hbm, *told],
-        [points_ref, ranks_ref, *(rows_ref.at[tile] for tile in range(tiles_count))],
-        small_sems,
-    )
-    copies = start_copies(kept_hbm, kept_refs, kept_sems)
-
-    def joined(index):
-        lanes = slice(index * group_len, (index + 1) * group_len)
-        return jnp.concatenate([packed_ref[group, :, lanes] for group in range(rhs_count)], axis=1)
-
-    columns = jnp.concatenate([joined(dim) for dim in range(dims)], axis=0).T
-    smalls[0].wait()
-    dist_sq = None
-    for dim in range(dims):
-        gap = columns[:, dim : dim + 1] - points_ref[dim : dim + 1, :]
-        dist_sq = gap * gap if dist_sq is None else dist_sq + gap * gap
-    cross = (jnp.exp(-2.0 * dist_sq) * amplitude).astype(jnp.bfloat16)
-    owner = joined(dims).astype(jnp.int32)
+    packed = jnp.concatenate([ref[...] for ref in cand_refs], axis=1)
+    owner = packed[dims:].astype(jnp.int32)
     hot = lax.broadcasted_iota(jnp.int32, (tiles_count, total), 0) == owner
     before = lax.broadcasted_iota(jnp.int32, (total, total), 0)
     after = lax.broadcasted_iota(jnp.int32, (total, total), 1)
@@ -219,13 +207,17 @@
     )
     within = jnp.sum(jnp.where(hot, counts, 0.0), axis=0, keepdims=True).astype(jnp.int32)
     piece = lax.broadcasted_iota(jnp.int32, (1, total), 1) // group_len
-    place = (within * tiles_count + owner) * rhs_count + piece
+    group = piece ^ lax.axis_index("rhs")
+    place = (within * tiles_count + owner) * rhs_count + group
     order = (before == place).astype(jnp.float32).astype(jnp.bfloat16)
+    columns = packed[:dims].T
+    dist_sq = None
+    for dim in range(dims):
+        gap = columns[:, dim : dim + 1] - points_ref[dim : dim + 1, :]
+        dist_sq = gap * gap if dist_sq is None else dist_sq + gap * gap
+    cross = (jnp.exp(-2.0 * dist_sq) * amplitude).astype(jnp.bfloat16)
     ordered = jnp.dot(order, cross, preferred_element_type=jnp.float32)
     cross_ref[...] = ordered.astype(jnp.bfloat16)
-    wait_for(smalls[1:])
-    plan_into(plan_ref, rows_ref, ranks_ref, (dims + 1) * group_len - first_lane)
-    wait_for(copies)
 
 
 def pair_at(plan_ref, u_ref, v_ref, shift):
@@ -337,24 +329,36 @@
     tiles_count = lax.axis_size("tiles")
     rhs_count = lax.axis_size("rhs")
     rows_here, block_len = rhs_rows.shape
-    slot_count, width = u_factors.shape[1], u_factors.shape[3]
-
-    inverse = {0: diag_inverse}
-    bit = rhs_count // 2
-    while bit > 1:
-        for d, piece in list(inverse.items()):
-            inverse[d ^ bit] = from_shard(piece, "rhs", rhs_count, bit)
-        bit //= 2
-    inverse[1] = from_shard(diag_inverse, "rhs", rhs_count, 1)
+    width = u_factors.shape[3]
+
     devices = tiles_count * rhs_count
     dims, group_len = cand_coords.shape
     total = rhs_count * group_len
-    lanes = -(-((dims + 1) * group_len + slot_count) // 128) * 128
-    packed = pl.pallas_call(
+
+    def resident(arrays):
+        return [pltpu.with_memory_space_constraint(array, pltpu.VMEM) for array in arrays]
+
+    def sent_far(held):
+        pieces, bit = {0: held}, rhs_count // 2
+        while bit > 1:
+            for d, piece in list(pieces.items()):
+                pieces[d ^ bit] = from_shard(piece, "rhs", rhs_count, bit)
+            bit //= 2
+        return pieces
+
+    def sent_on(pieces):
+        for d in [d for d in pieces if d > 1]:
+            pieces[d ^ 1] = from_shard(pieces[d], "rhs", rhs_count, 1)
+
+    inverse = sent_far(diag_inverse)
+    listed, packed = pl.pallas_call(
         pack_kernel,
-        out_shape=jax.ShapeDtypeStruct((devices, 1, lanes), jnp.float32),
+        out_shape=(
+            jax.ShapeDtypeStruct((tiles_count, 1, 128), jnp.int32),
+            jax.ShapeDtypeStruct((dims + 1, group_len), jnp.float32),
+        ),
         in_specs=[HBM] * 3,
-        out_specs=VMEM,
+        out_specs=(VMEM, VMEM),
         compiler_params=PARAMS,
         scratch_shapes=[
             pltpu.VMEM(cand_coords.shape, jnp.float32),
@@ -363,43 +367,54 @@
             pltpu.SemaphoreType.DMA((3,)),
         ],
     )(in_hbm(cand_coords), in_hbm(owner[None, :]), in_hbm(tile_rows))
-    told = lax.all_to_all(packed, ("tiles", "rhs"), 0, 0, tiled=True)
+    beside = from_shard(packed, "rhs", rhs_count, 1)
+    told = lax.all_to_all(listed, "tiles", 0, 0, tiled=True)
+    early = (rhs_rows, v_factors[0], point_coords)
+    rhs_kept, v_kept, points_kept = pl.pallas_call(
+        load_kernel,
+        out_shape=[pltpu.VMEM(array.shape, array.dtype) for array in early],
+        in_specs=[HBM] * len(early),
+        out_specs=[VMEM] * len(early),
+        compiler_params=PARAMS,
+        scratch_shapes=[pltpu.SemaphoreType.DMA((len(early),))],
+    )(*(in_hbm(array) for array in early))
+    beside, rhs_kept = lax.optimization_barrier((beside, rhs_kept))
+    inverse[1] = from_shard(diag_inverse, "rhs", rhs_count, 1)
+    cand = sent_far(packed)
+    cand.update({d ^ 1: piece for d, piece in sent_far(beside).items()})
     amplitude = 4.0 / math.sqrt(block_len * tiles_count)
-    pieces_far = [d for d in inverse if d > 1]
-    held, told = lax.optimization_barrier(([inverse[d] for d in pieces_far], told))
-    for d, piece in zip(pieces_far, held, strict=True):
-        inverse[d] = piece
-        inverse[d ^ 1] = from_shard(piece, "rhs", rhs_count, 1)
-    loaded = (rhs_rows, u_factors[0], v_factors[0], diag_inverse)
-    table_lanes = lanes - (dims + 1) * group_len // 128 * 128
-    plan, cross, *kept, own_piece = pl.pallas_call(
-        functools.partial(
-            prepare_kernel, amplitude=amplitude, group_len=group_len, kept_count=len(loaded)
+    cross = pl.pallas_call(
+        functools.partial(cross_kernel, amplitude=amplitude, tiles_count=tiles_count),
+        out_shape=pltpu.VMEM((total, block_len), jnp.bfloat16),
+        in_specs=[VMEM] * (1 + rhs_count),
+        out_specs=VMEM,
+        compiler_params=PARAMS,
+    )(resident([points_kept])[0], *(cand[d] for d in range(rhs_count)))
+    sent_on(inverse)
+    plan, u_kept, own_piece = pl.pallas_call(
+        plan_kernel,
+        out_shape=(
+            pltpu.SMEM((5, tiles_count), jnp.int32),
+            pltpu.VMEM(u_factors.shape[1:], u_factors.dtype),
+            pltpu.VMEM(diag_inverse.shape, diag_inverse.dtype),
         ),
-        out_shape=(
-            jax.ShapeDtypeStruct((5, tiles_count), jnp.int32),
-            jax.ShapeDtypeStruct((total, block_len), jnp.bfloat16),
-            *(pltpu.VMEM(array.shape, array.dtype) for array in loaded),
-        ),
-        in_specs=[VMEM] + [HBM] * (2 + len(loaded)),
-        out_specs=(SMEM, *[VMEM] * (1 + len(loaded))),
+        in_specs=[VMEM] + [HBM] * 3,
+        out_specs=(SMEM, VMEM, VMEM),
         compiler_params=PARAMS,
         scratch_shapes=[
+            pltpu.SMEM((tiles_count, 1, 128), jnp.int32),
             pltpu.SMEM(tile_ranks.shape, jnp.int32),
-            pltpu.VMEM(point_coords.shape, jnp.float32),
-            pltpu.SMEM((tiles_count, 1, table_lanes), jnp.float32),
-            pltpu.SemaphoreType.DMA((len(loaded),)),
-            pltpu.SemaphoreType.DMA((2 + tiles_count,)),
+            pltpu.SemaphoreType.DMA((4,)),
         ],
-    )(told, *(in_hbm(array) for array in (tile_ranks, point_coords, *loaded)))
-
-    def resident(arrays):
-        return [pltpu.with_memory_space_constraint(array, pltpu.VMEM) for array in arrays]
+    )(told, in_hbm(tile_ranks), in_hbm(u_factors[0]), in_hbm(diag_inverse))
+    cross, plan = lax.optimization_barrier((cross, plan))
+
+    plan = pltpu.with_memory_space_constraint(plan, pltpu.SMEM)
 
     def weights():
-        return resident(kept), resident([own_piece, *(inverse[d] for d in range(1, rhs_count))])
-
-    sent = jax.ShapeDtypeStruct((tiles_count, rows_here, 2 * width), jnp.bfloat16)
+        return resident([rhs_kept, u_kept, v_kept]), resident([own_piece, *(inverse[d] for d in range(1, rhs_count))])
+
+    sent = pltpu.VMEM((tiles_count, rows_here, 2 * width), jnp.bfloat16)
     rounded = jax.ShapeDtypeStruct((rows_here, block_len), jnp.bfloat16)
     block = pltpu.VMEM(rounded.shape, jnp.bfloat16)
     wide = pltpu.VMEM(rounded.shape, jnp.float32)
@@ -434,7 +449,7 @@
         last_kernel,
         out_shape=(
             rounded,
-            jax.ShapeDtypeStruct((devices, 1, owned * rows_here), jnp.float32),
+            pltpu.VMEM((devices, 1, owned * rows_here), jnp.float32),
         ),
         in_specs=[SMEM] + [VMEM] * (5 + rhs_count),
         out_specs=(VMEM, VMEM),

time: 66.6 us -> 75.8 us (1.14)
  waiting for transfers between devices: 7.19 us -> 15.3 us
  starting transfers between devices: 8.28 us -> 11.4 us
  blocking collectives: 37.3 us -> 35.3 us
  Pallas kernels: 12.9 us -> 12 us
    ppermute x3 -> x6, waiting for transfers between devices: 0.01 us -> 15.3 us  [from_shard(): return lax.ppermute(piece, axis, xor_pairs(size, bit))]
    all_to_all x1, waiting for transfers between devices: 7.18 us -> 0.01 us  [dense_device(): told = lax.all_to_all(listed, 'tiles', 0, 0, tiled=True)]
    ppermute x3 -> x6, starting transfers between devices: 3.35 us -> 5.35 us  [from_shard(): return lax.ppermute(piece, axis, xor_pairs(size, bit))]
    all_to_all x1, starting transfers between devices: 4.93 us -> 6.09 us  [dense_device(): told = lax.all_to_all(listed, 'tiles', 0, 0, tiled=True)]
    all_to_all x2, blocking collectives: 26.7 us -> 25.7 us  [exchange(): return lax.all_to_all(send, 'tiles', 0, 0, tiled=True)]
    all_to_all x1, blocking collectives: 10.6 us -> 9.63 us  [dense_device(): parts = lax.all_to_all(partial_values, ('tiles', 'rhs'), 0, 0, tiled=True)]
    pallas_call x3 -> x5, Pallas kernels: 7.28 us -> 7.65 us  [the longest x1 2.22 us: dense_device(): pl.pallas_call(last_kernel, out_shape=(rounded, pltpu.VMEM((devices, 1, o...]
  transfers between devices with their start and end apart: 4 -> 7, of which waited for: 1 -> 2; matrix products, arithmetic and copies ran while one was open for 0% -> 0% of each run, Pallas kernels for 7% -> 7%
where the time goes in v2:
time: 75.8 us; the launch traced here: 75.4 us
  blocking collectives  35.3 us (47%)
  waiting for transfers between devices  15.3 us (20%)
  Pallas kernels  12 us (16%)
  starting transfers between devices  11.4 us (15%)
    all_to_all x2, blocking collectives, exchange(): return lax.all_to_all(send, 'tiles', 0, 0, tiled=True)  25.7 us
    ppermute x6, waiting for transfers between devices, from_shard(): return lax.ppermute(piece, axis, xor_pairs(size, bit))  15.3 us
    all_to_all x1, blocking collectives, dense_device(): parts = lax.all_to_all(partial_values, ('tiles', 'rhs'), 0, 0, tiled=True)  9.63 us
    all_to_all x1, starting transfers between devices, dense_device(): told = lax.all_to_all(listed, 'tiles', 0, 0, tiled=True)  6.09 us
    ppermute x6, starting transfers between devices, from_shard(): return lax.ppermute(piece, axis, xor_pairs(size, bit))  5.35 us
    pallas_call x1, Pallas kernels, dense_device(): pl.pallas_call(middle_kernel, out_shape=sent, in_specs=[SMEM] + [VMEM] *...  2.35 us
    pallas_call x1, Pallas kernels, dense_device(): pl.pallas_call(last_kernel, out_shape=(rounded, pltpu.VMEM((devices, 1, o...  2.22 us
    pallas_call x1, Pallas kernels, dense_device(): pl.pallas_call(plan_kernel, out_shape=(pltpu.SMEM((5, tiles_count), jnp.i...  1.63 us
  transfers between devices with their start and end apart: 7, of which 2 were waited for; matrix products, arithmetic and copies ran while one was open for 0% of the time, Pallas kernels for 7%

profile of v2, /device:TPU:0, one launch (start us, length us, event | category | flops | bytes accessed | tf_op | source)
XLA Modules:
  0.0 75.4 jit_solution(16584414444259783756)
XLA Ops:
  0.6 3.0 %collective-permute-start.4 = (bf16[1024,256]{1,0:T(8,128)(2,1)}, bf16[1024,256]{1,0:T(8,128)(2,1)S(1)}, u32[]{:S(2)}, u32[]{:S(2)}) collective-permute-start(bf16[1024,256]{1,0:T(8,128)(2,1)} %own_hbm.1), channel_id=1, source_target_pairs={{0,2},{1,3},{2,0},{3,1},{4,6},{5,7},{6,4},{7,5},{8,10},{9,11},{10,... | collective-permute-start | bytes 1572872 | tf_op jit(solution)/shard_map/ppermute | solution.py:119
  3.7 0.0 collective-permute-start.3
  3.7 12.1 %collective-permute-done.4.refs_2_ = bf16[1024,256]{1,0:T(8,128)(2,1)S(1)} collective-permute-done((bf16[1024,256]{1,0:T(8,128)(2,1)}, bf16[1024,256]{1,0:T(8,128)(2,1)S(1)}, u32[]{:S(2)}, u32[]{:S(2)}) %collective-permute-start.4) | collective-permute-done | bytes 524320 | tf_op jit(solution)/shard_map/ppermute | solution.py:119
  15.8 0.0 collective-permute-start.5
  15.8 1.3 %shard_map.105 = (s32[8,1,128]{2,1,0:T(1,128)}, f32[9,32]{1,0:T(8,128)S(1)}) custom-call(f32[8,32]{1,0:T(8,128)} %cand_hbm.1, s32[1,32]{1,0:T(1,128)} %bitcast.5, s32[1,7]{1,0:T(1,128)} %rows_hbm.1), custom_call_target="tpu_custom_call" | custom-call | tf_op jit(solution)/shard_map/pallas_call | solution.py:354
  17.1 6.1 %all-to-all-start = ((s32[8,1,128]{2,1,0:T(1,128)}), s32[8,1,128]{2,1,0:T(1,128)S(1)}, u32[]{:S(2)}, u32[]{:S(2)}) async-start(s32[8,1,128]{2,1,0:T(1,128)} %get-tuple-element.20), calls=%async_computation | async-start | bytes 8192 | tf_op jit(solution)/shard_map/all_to_all | solution.py:371
  23.2 0.2 collective-permute-start
  23.4 1.5 %collective-permute-start.1 = (f32[9,32]{1,0:T(8,128)S(1)}, f32[9,32]{1,0:T(8,128)S(1)}, u32[]{:S(2)}, u32[]{:S(2)}) collective-permute-start(f32[9,32]{1,0:T(8,128)S(1)} %get-tuple-element.17.refs_0_), channel_id=1, source_target_pairs={{0,2},{1,3},{2,0},{3,1},{4,6},{5,7},{6,4},{7,5},{8,10},{9,11},{10,... | collective-permute-start | bytes 3464 | tf_op jit(solution)/shard_map/ppermute | solution.py:119
  24.9 1.6 %shard_map.104 = (bf16[64,1024]{1,0:T(8,128)(2,1)S(1)}, bf16[7,1024,128]{2,1,0:T(8,128)(2,1)S(1)}, f32[8,1024]{1,0:T(8,128)S(1)}) custom-call(bf16[64,1024]{1,0:T(8,128)(2,1)} %refs_0_.1, bf16[7,1024,128]{2,1,0:T(8,128)(2,1)} %bitcast.3, f32[8,1024]{1,0:T(8,128)} %refs_2_.1), custom_call_target="tpu_custom_call" | custom-call | tf_op jit(solution)/shard_map/pallas_call | solution.py:373
  26.5 0.0 collective-permute-done.refs_1_
  26.6 0.6 collective-permute-start.2
  27.2 0.0 collective-permute-done.1.refs_2_
  27.2 3.1 %collective-permute-done.2.refs_3_ = f32[9,32]{1,0:T(8,128)S(1)} collective-permute-done((f32[9,32]{1,0:T(8,128)S(1)}, f32[9,32]{1,0:T(8,128)S(1)}, u32[]{:S(2)}, u32[]{:S(2)}) %collective-permute-start.2) | collective-permute-done | bytes 1184 | tf_op jit(solution)/shard_map/ppermute | solution.py:119
  30.3 0.9 %shard_map.106.cross_ref = bf16[128,1024]{1,0:T(8,128)(2,1)S(1)} custom-call(f32[8,1024]{1,0:T(8,128)S(1)} %get-tuple-element.16.points_ref, f32[9,32]{1,0:T(8,128)S(1)} %get-tuple-element.17.refs_0_, f32[9,32]{1,0:T(8,128)S(1)} %collective-permute-done.refs_1_, f32[9,32]{1,0:T(8,128)S(1)} %collective-permute-done.1.refs_2_, ...), custom_call_target="tpu_custom_call" | custom-call | tf_op jit(solution)/shard_map/pallas_call | solution.py:386
  31.2 0.0 copy-start
  31.2 0.7 copy-done
  31.9 0.0 all-to-all-done.listed_in
  31.9 1.6 %shard_map.107 = (s32[5,8]{1,0:T(8,128)S(4)}, bf16[7,1024,128]{2,1,0:T(8,128)(2,1)S(1)}, bf16[1024,256]{1,0:T(8,128)(2,1)S(1)}) custom-call(s32[8,1,128]{2,1,0:T(1,128)S(1)} %all-to-all-done.listed_in, s32[1,7]{1,0:T(1,128)} %ranks_hbm.1, bf16[7,1024,128]{2,1,0:T(8,128)(2,1)} %bitcast.4, bf16[1024,256]{1,0:T(8,128)(2,1)} %own_hbm.1), custom_call_target="tpu_custom_call" | custom-call | tf_op jit(solution)/shard_map/pallas_call | solution.py:394
  33.5 0.0 collective-permute-done.3.refs_1_
  33.5 0.0 collective-permute-done.5.refs_3_
  33.5 1.3 %shard_map.108 = bf16[8,64,256]{2,1,0:T(8,128)(2,1)S(1)} custom-call(s32[5,8]{1,0:T(8,128)S(4)} %get-tuple-element.22.plan_ref, bf16[64,1024]{1,0:T(8,128)(2,1)S(1)} %get-tuple-element.23.rhs_ref, bf16[7,1024,128]{2,1,0:T(8,128)(2,1)S(1)} %get-tuple-element.24.u_ref, bf16[7,1024,128]{2,1,0:T(8,128)(2,1)S(1)} %get-tuple-element.25.v_ref, ...), custom_call_target="tpu_custom_call" | custom-call | tf_op jit(solution)/shard_map/pallas_call | solution.py:426
  34.9 13.9 %all_to_all.20.recv_ref = bf16[8,64,256]{2,1,0:T(8,128)(2,1)S(1)} all-to-all(bf16[8,64,256]{2,1,0:T(8,128)(2,1)S(1)} %shard_map.108), channel_id=1, replica_groups=mesh['tiles'=8,'rhs'=4] {'tiles'}, dimensions={0} | all-to-all | bytes 524288 | tf_op jit(solution)/shard_map/all_to_all | solution.py:423
  48.8 0.0 copy-start.1
  48.8 2.4 %shard_map.109 = bf16[8,64,256]{2,1,0:T(8,128)(2,1)S(1)} custom-call(s32[5,8]{1,0:T(8,128)S(4)} %get-tuple-element.22.plan_ref, bf16[8,64,256]{2,1,0:T(8,128)(2,1)S(1)} %all_to_all.20.recv_ref, bf16[64,1024]{1,0:T(8,128)(2,1)S(1)} %get-tuple-element.23.rhs_ref, bf16[7,1024,128]{2,1,0:T(8,128)(2,1)S(1)} %get-tuple-element.24.u_ref, ...), custom_call_target="tpu_custom_call" | custom-call | tf_op jit(solution)/shard_map/pallas_call | solution.py:437
  51.1 11.8 %all_to_all.21.recv_ref = bf16[8,64,256]{2,1,0:T(8,128)(2,1)S(1)} all-to-all(bf16[8,64,256]{2,1,0:T(8,128)(2,1)S(1)} %shard_map.109), channel_id=1, replica_groups=mesh['tiles'=8,'rhs'=4] {'tiles'}, dimensions={0} | all-to-all | bytes 524288 | tf_op jit(solution)/shard_map/all_to_all | solution.py:423
  62.9 0.0 copy-done.1
  62.9 2.2 %shard_map.110 = (bf16[64,1024]{1,0:T(8,128)(2,1)}, f32[32,1,256]{2,1,0:T(1,128)S(1)}) custom-call(s32[5,8]{1,0:T(8,128)S(4)} %get-tuple-element.22.plan_ref, bf16[8,64,256]{2,1,0:T(8,128)(2,1)S(1)} %all_to_all.21.recv_ref, bf16[64,1024]{1,0:T(8,128)(2,1)S(1)} %get-tuple-element.23.rhs_ref, bf16[7,1024,128]{2,1,0:T(8,128)(2,1)S(1)} %get-tuple-element.24.u_ref, ...), custom_call_target="tpu_custom_call" | custom-call | tf_op jit(solution)/shard_map/pallas_call | solution.py:448
  65.1 9.6 %all_to_all.22.parts_ref = f32[32,1,256]{2,1,0:T(1,128)S(1)} all-to-all(f32[32,1,256]{2,1,0:T(1,128)S(1)} %get-tuple-element.29), channel_id=1, replica_groups=mesh['tiles'=8,'rhs'=4] {'tiles','rhs'}, dimensions={0} | all-to-all | bytes 65536 | tf_op jit(solution)/shard_map/all_to_all | solution.py:459
  74.7 0.7 shard_map.111
Async XLA Ops:
  0.6 15.2 %collective-permute-start.4 = (bf16[1024,256]{1,0:T(8,128)(2,1)}, bf16[1024,256]{1,0:T(8,128)(2,1)S(1)}, u32[]{:S(2)}, u32[]{:S(2)}) collective-permute-start(bf16[1024,256]{1,0:T(8,128)(2,1)} %own_hbm.1), channel_id=1, source_target_pairs={{0,2},{1,3},{2,0},{3,1},{4,6},{5,7},{6,4},{7,5},{8,10},{9,11},{10,... | collective-permute-start | bytes 1572872 | tf_op jit(solution)/shard_map/ppermute | solution.py:119
  3.7 29.8 %collective-permute-start.3 = (bf16[1024,256]{1,0:T(8,128)(2,1)}, bf16[1024,256]{1,0:T(8,128)(2,1)S(1)}, u32[]{:S(2)}, u32[]{:S(2)}) collective-permute-start(bf16[1024,256]{1,0:T(8,128)(2,1)} %own_hbm.1), channel_id=1, source_target_pairs={{0,1},{1,0},{2,3},{3,2},{4,5},{5,4},{6,7},{7,6},{8,9},{9,8},{10,11... | collective-permute-start | bytes 1572872 | tf_op jit(solution)/shard_map/ppermute | solution.py:119
  15.8 17.7 %collective-permute-start.5 = (bf16[1024,256]{1,0:T(8,128)(2,1)S(1)}, bf16[1024,256]{1,0:T(8,128)(2,1)S(1)}, u32[]{:S(2)}, u32[]{:S(2)}) collective-permute-start(bf16[1024,256]{1,0:T(8,128)(2,1)S(1)} %collective-permute-done.4.refs_2_), channel_id=1, source_target_pairs={{0,1},{1,0},{2,3},{3,2},{4,5},{5,4},{6,7},{7,6},{8,9},{9,8},{10,11... | collective-permute-start | bytes 1572872 | tf_op jit(solution)/shard_map/ppermute | solution.py:119
  17.1 14.7 %all-to-all-start = ((s32[8,1,128]{2,1,0:T(1,128)}), s32[8,1,128]{2,1,0:T(1,128)S(1)}, u32[]{:S(2)}, u32[]{:S(2)}) async-start(s32[8,1,128]{2,1,0:T(1,128)} %get-tuple-element.20), calls=%async_computation | async-start | bytes 8192 | tf_op jit(solution)/shard_map/all_to_all | solution.py:371
  23.2 3.3 %collective-permute-start = (f32[9,32]{1,0:T(8,128)S(1)}, f32[9,32]{1,0:T(8,128)S(1)}, u32[]{:S(2)}, u32[]{:S(2)}) collective-permute-start(f32[9,32]{1,0:T(8,128)S(1)} %get-tuple-element.17.refs_0_), channel_id=1, source_target_pairs={{0,1},{1,0},{2,3},{3,2},{4,5},{5,4},{6,7},{7,6},{8,9},{9,8},{10,11... | collective-permute-start | bytes 3464 | tf_op jit(solution)/shard_map/ppermute | solution.py:119
  23.4 3.7 %collective-permute-start.1 = (f32[9,32]{1,0:T(8,128)S(1)}, f32[9,32]{1,0:T(8,128)S(1)}, u32[]{:S(2)}, u32[]{:S(2)}) collective-permute-start(f32[9,32]{1,0:T(8,128)S(1)} %get-tuple-element.17.refs_0_), channel_id=1, source_target_pairs={{0,2},{1,3},{2,0},{3,1},{4,6},{5,7},{6,4},{7,5},{8,10},{9,11},{10,... | collective-permute-start | bytes 3464 | tf_op jit(solution)/shard_map/ppermute | solution.py:119
  26.6 3.7 %collective-permute-start.2 = (f32[9,32]{1,0:T(8,128)S(1)}, f32[9,32]{1,0:T(8,128)S(1)}, u32[]{:S(2)}, u32[]{:S(2)}) collective-permute-start(f32[9,32]{1,0:T(8,128)S(1)} %collective-permute-done.refs_1_), channel_id=1, source_target_pairs={{0,2},{1,3},{2,0},{3,1},{4,6},{5,7},{6,4},{7,5},{8,10},{9,11},{10,... | collective-permute-start | bytes 3464 | tf_op jit(solution)/shard_map/ppermute | solution.py:119
  31.2 0.7 copy-start
  48.8 14.1 %copy-start.1 = (bf16[128,1024]{1,0:T(8,128)(2,1)S(1)}, bf16[128,1024]{1,0:T(8,128)(2,1)}, u32[]{:S(2)}) copy-start(bf16[128,1024]{1,0:T(8,128)(2,1)} %copy-done) | copy-start | bytes 786436

commit v3 on v2

--- a/solution.py
+++ b/solution.py
@@ -269,10 +269,47 @@
     resid_ref[...] = (rhs_ref[...].astype(jnp.float32) - total_ref[...]).astype(jnp.bfloat16)
 
 
-def first_kernel(plan_ref, rhs_ref, u_ref, v_ref, *refs):
-    inverse_refs, (send_ref, iterate_ref) = refs[:-2], refs[-2:]
-    precondition_into(rhs_ref[...], inverse_refs, plan_ref[4, 0], iterate_ref)
-    store_products(iterate_ref[...], u_ref, v_ref, send_ref, plan_ref)
+def columns_product(plan_ref, rhs_ref, u_ref, v_ref, inverse_refs, places):
+    resid = rhs_ref[...]
+    columns = inverse_refs[0].shape[1]
+    iterate = jnp.concatenate(
+        [
+            jnp.dot(resid, ref[...], preferred_element_type=jnp.float32).astype(jnp.bfloat16)
+            for ref in inverse_refs
+        ],
+        axis=1,
+    )
+    rows = [
+        pl.ds(pl.multiple_of((plan_ref[4, 0] ^ d) * columns, columns), columns) for d in places
+    ]
+    for shift in range(1, plan_ref.shape[1]):
+        out_slot, in_slot = plan_ref[1, shift], plan_ref[2, shift]
+        factors = [
+            jnp.concatenate([v_ref[out_slot, at, :], u_ref[in_slot, at, :]], axis=1) for at in rows
+        ]
+        yield shift, jnp.dot(
+            iterate, jnp.concatenate(factors, axis=0), preferred_element_type=jnp.float32
+        )
+
+
+def early_kernel(plan_ref, rhs_ref, u_ref, v_ref, *refs, places):
+    inverse_refs, sums_ref = refs[:-1], refs[-1]
+    products = columns_product(plan_ref, rhs_ref, u_ref, v_ref, inverse_refs, places)
+    for shift, product in products:
+        sums_ref[shift - 1] = product
+
+
+def first_kernel(plan_ref, rhs_ref, u_ref, v_ref, sums_ref, *refs, places):
+    inverse_refs, send_ref = refs[:-1], refs[-1]
+    width = u_ref.shape[2]
+    products = columns_product(plan_ref, rhs_ref, u_ref, v_ref, inverse_refs, places)
+    for shift, product in products:
+        product += sums_ref[shift - 1]
+        there = plan_ref[0, shift]
+        lower = jnp.where(rank_mask(plan_ref, shift, width), product[:, :width], 0.0)
+        send_ref[there, :, :width] = lower.astype(jnp.bfloat16)
+        send_ref[there, :, width:] = product[:, width:].astype(jnp.bfloat16)
+    send_ref[plan_ref[0, 0]] = jnp.zeros(send_ref.shape[1:], jnp.bfloat16)
 
 
 def middle_kernel(plan_ref, recv_ref, rhs_ref, u_ref, v_ref, *refs):
@@ -422,15 +459,24 @@
     def exchange(send):
         return lax.all_to_all(send, "tiles", 0, 0, tiled=True)
 
+    late = [d for d in range(rhs_count) if d > 1 and d % 2]
+    soon = [d for d in range(rhs_count) if d not in late]
+    kept, pieces = weights()
+    sums = pl.pallas_call(
+        functools.partial(early_kernel, places=soon),
+        out_shape=pltpu.VMEM((tiles_count - 1, rows_here, 2 * width), jnp.float32),
+        in_specs=[SMEM] + [VMEM] * (3 + len(soon)),
+        out_specs=VMEM,
+        compiler_params=PARAMS,
+    )(plan, *kept, *(pieces[d] for d in soon))
     kept, pieces = weights()
     send = pl.pallas_call(
-        first_kernel,
+        functools.partial(first_kernel, places=late),
         out_shape=sent,
-        in_specs=[SMEM] + [VMEM] * (3 + rhs_count),
+        in_specs=[SMEM] + [VMEM] * (4 + len(late)),
         out_specs=VMEM,
         compiler_params=PARAMS,
-        scratch_shapes=[block],
-    )(plan, *kept, *pieces)
+    )(plan, *kept, *resident([sums]), *(pieces[d] for d in late))
     for _ in range(ITERS - 1):
         recv = exchange(send)
         kept, pieces = weights()
@@ -468,7 +514,7 @@
 
 
 def takes_dense(slot_count, tiles_count, rhs_count):
-    return slot_count == tiles_count - 1 and rhs_count > 1 and rhs_count & (rhs_count - 1) == 0
+    return slot_count == tiles_count - 1 and rhs_count > 2 and rhs_count & (rhs_count - 1) == 0
 
 
 def per_device(rhs_rows, diag_inverse, u_factors, *others):

time: 75.8 us -> 76 us (level)
    pallas_call x1 -> x2, Pallas kernels: 1.34 us -> 1.58 us  [the longest x1 0.99 us: dense_device(): pl.pallas_call(functools.partial(early_kernel, places=soon), out_shape=pl...]
  transfers between devices with their start and end apart: 7 -> 7, of which waited for: 2 -> 2; matrix products, arithmetic and copies ran while one was open for 0% -> 0% of each run, Pallas kernels for 7% -> 8%
where the time goes in v3:
time: 76 us; the launch traced here: 75.6 us
  blocking collectives  35.3 us (46%)
  waiting for transfers between devices  15.3 us (20%)
  Pallas kernels  12.3 us (16%)
  starting transfers between devices  11.4 us (15%)
    all_to_all x2, blocking collectives, exchange(): return lax.all_to_all(send, 'tiles', 0, 0, tiled=True)  25.6 us
    ppermute x6, waiting for transfers between devices, from_shard(): return lax.ppermute(piece, axis, xor_pairs(size, bit))  15.3 us
    all_to_all x1, blocking collectives, dense_device(): parts = lax.all_to_all(partial_values, ('tiles', 'rhs'), 0, 0, tiled=True)  9.63 us
    all_to_all x1, starting transfers between devices, dense_device(): told = lax.all_to_all(listed, 'tiles', 0, 0, tiled=True)  6.09 us
    ppermute x6, starting transfers between devices, from_shard(): return lax.ppermute(piece, axis, xor_pairs(size, bit))  5.35 us
    pallas_call x1, Pallas kernels, dense_device(): pl.pallas_call(middle_kernel, out_shape=sent, in_specs=[SMEM] + [VMEM] *...  2.35 us
    pallas_call x1, Pallas kernels, dense_device(): pl.pallas_call(last_kernel, out_shape=(rounded, pltpu.VMEM((devices, 1, o...  2.22 us
    pallas_call x1, Pallas kernels, dense_device(): pl.pallas_call(plan_kernel, out_shape=(pltpu.SMEM((5, tiles_count), jnp.i...  1.63 us
  transfers between devices with their start and end apart: 7, of which 2 were waited for; matrix products, arithmetic and copies ran while one was open for 0% of the time, Pallas kernels for 8%

profile of v3, /device:TPU:0, one launch (start us, length us, event | category | flops | bytes accessed | tf_op | source)
XLA Modules:
  0.0 75.6 jit_solution(12766351872307492520)
XLA Ops:
  0.6 3.0 %collective-permute-start.4 = (bf16[1024,256]{1,0:T(8,128)(2,1)}, bf16[1024,256]{1,0:T(8,128)(2,1)S(1)}, u32[]{:S(2)}, u32[]{:S(2)}) collective-permute-start(bf16[1024,256]{1,0:T(8,128)(2,1)} %own_hbm.1), channel_id=1, source_target_pairs={{0,2},{1,3},{2,0},{3,1},{4,6},{5,7},{6,4},{7,5},{8,10},{9,11},{10,... | collective-permute-start | bytes 1572872 | tf_op jit(solution)/shard_map/ppermute | solution.py:119
  3.7 0.0 collective-permute-start.3
  3.7 12.1 %collective-permute-done.4.refs_2_ = bf16[1024,256]{1,0:T(8,128)(2,1)S(1)} collective-permute-done((bf16[1024,256]{1,0:T(8,128)(2,1)}, bf16[1024,256]{1,0:T(8,128)(2,1)S(1)}, u32[]{:S(2)}, u32[]{:S(2)}) %collective-permute-start.4) | collective-permute-done | bytes 524320 | tf_op jit(solution)/shard_map/ppermute | solution.py:119
  15.8 0.0 collective-permute-start.5
  15.8 1.3 %shard_map.105 = (s32[8,1,128]{2,1,0:T(1,128)}, f32[9,32]{1,0:T(8,128)S(1)}) custom-call(f32[8,32]{1,0:T(8,128)} %cand_hbm.1, s32[1,32]{1,0:T(1,128)} %bitcast.5, s32[1,7]{1,0:T(1,128)} %rows_hbm.1), custom_call_target="tpu_custom_call" | custom-call | tf_op jit(solution)/shard_map/pallas_call | solution.py:391
  17.1 6.1 %all-to-all-start = ((s32[8,1,128]{2,1,0:T(1,128)}), s32[8,1,128]{2,1,0:T(1,128)S(1)}, u32[]{:S(2)}, u32[]{:S(2)}) async-start(s32[8,1,128]{2,1,0:T(1,128)} %get-tuple-element.20), calls=%async_computation | async-start | bytes 8192 | tf_op jit(solution)/shard_map/all_to_all | solution.py:408
  23.2 0.2 collective-permute-start
  23.4 1.5 %collective-permute-start.1 = (f32[9,32]{1,0:T(8,128)S(1)}, f32[9,32]{1,0:T(8,128)S(1)}, u32[]{:S(2)}, u32[]{:S(2)}) collective-permute-start(f32[9,32]{1,0:T(8,128)S(1)} %get-tuple-element.17.refs_0_), channel_id=1, source_target_pairs={{0,2},{1,3},{2,0},{3,1},{4,6},{5,7},{6,4},{7,5},{8,10},{9,11},{10,... | collective-permute-start | bytes 3464 | tf_op jit(solution)/shard_map/ppermute | solution.py:119
  24.9 1.6 %shard_map.104 = (bf16[64,1024]{1,0:T(8,128)(2,1)S(1)}, bf16[7,1024,128]{2,1,0:T(8,128)(2,1)S(1)}, f32[8,1024]{1,0:T(8,128)S(1)}) custom-call(bf16[64,1024]{1,0:T(8,128)(2,1)} %refs_0_.1, bf16[7,1024,128]{2,1,0:T(8,128)(2,1)} %bitcast.3, f32[8,1024]{1,0:T(8,128)} %refs_2_.1), custom_call_target="tpu_custom_call" | custom-call | tf_op jit(solution)/shard_map/pallas_call | solution.py:410
  26.5 0.0 collective-permute-done.refs_1_
  26.6 0.6 collective-permute-start.2
  27.2 0.0 collective-permute-done.1.refs_2_
  27.2 3.1 %collective-permute-done.2.refs_3_ = f32[9,32]{1,0:T(8,128)S(1)} collective-permute-done((f32[9,32]{1,0:T(8,128)S(1)}, f32[9,32]{1,0:T(8,128)S(1)}, u32[]{:S(2)}, u32[]{:S(2)}) %collective-permute-start.2) | collective-permute-done | bytes 1184 | tf_op jit(solution)/shard_map/ppermute | solution.py:119
  30.3 0.9 %shard_map.106.cross_ref = bf16[128,1024]{1,0:T(8,128)(2,1)S(1)} custom-call(f32[8,1024]{1,0:T(8,128)S(1)} %get-tuple-element.16.points_ref, f32[9,32]{1,0:T(8,128)S(1)} %get-tuple-element.17.refs_0_, f32[9,32]{1,0:T(8,128)S(1)} %collective-permute-done.refs_1_, f32[9,32]{1,0:T(8,128)S(1)} %collective-permute-done.1.refs_2_, ...), custom_call_target="tpu_custom_call" | custom-call | tf_op jit(solution)/shard_map/pallas_call | solution.py:423
  31.2 0.0 copy-start
  31.2 0.7 copy-done
  31.9 0.0 all-to-all-done.listed_in
  31.9 1.6 %shard_map.107 = (s32[5,8]{1,0:T(8,128)S(4)}, bf16[7,1024,128]{2,1,0:T(8,128)(2,1)S(1)}, bf16[1024,256]{1,0:T(8,128)(2,1)S(1)}) custom-call(s32[8,1,128]{2,1,0:T(1,128)S(1)} %all-to-all-done.listed_in, s32[1,7]{1,0:T(1,128)} %ranks_hbm.1, bf16[7,1024,128]{2,1,0:T(8,128)(2,1)} %bitcast.4, bf16[1024,256]{1,0:T(8,128)(2,1)} %own_hbm.1), custom_call_target="tpu_custom_call" | custom-call | tf_op jit(solution)/shard_map/pallas_call | solution.py:431
  33.5 0.0 collective-permute-done.3.refs_1_
  33.5 1.0 %shard_map.108.sums_ref = f32[7,64,256]{2,1,0:T(8,128)S(1)} custom-call(s32[5,8]{1,0:T(8,128)S(4)} %get-tuple-element.22.plan_ref, bf16[64,1024]{1,0:T(8,128)(2,1)S(1)} %get-tuple-element.23.rhs_ref, bf16[7,1024,128]{2,1,0:T(8,128)(2,1)S(1)} %get-tuple-element.24.u_ref, bf16[7,1024,128]{2,1,0:T(8,128)(2,1)S(1)} %get-tuple-element.25.v_ref, ...), custom_call_target="tpu_custom_call" | custom-call | tf_op jit(solution)/shard_map/pallas_call | solution.py:465
  34.5 0.0 collective-permute-done.5.refs_0_.refs_3_
  34.5 0.6 shard_map.109
  35.1 13.9 %all_to_all.20.recv_ref = bf16[8,64,256]{2,1,0:T(8,128)(2,1)S(1)} all-to-all(bf16[8,64,256]{2,1,0:T(8,128)(2,1)S(1)} %shard_map.109), channel_id=1, replica_groups=mesh['tiles'=8,'rhs'=4] {'tiles'}, dimensions={0} | all-to-all | bytes 524288 | tf_op jit(solution)/shard_map/all_to_all | solution.py:460
  49.0 0.0 copy-start.1
  49.0 2.4 %shard_map.110 = bf16[8,64,256]{2,1,0:T(8,128)(2,1)S(1)} custom-call(s32[5,8]{1,0:T(8,128)S(4)} %get-tuple-element.22.plan_ref, bf16[8,64,256]{2,1,0:T(8,128)(2,1)S(1)} %all_to_all.20.recv_ref, bf16[64,1024]{1,0:T(8,128)(2,1)S(1)} %get-tuple-element.23.rhs_ref, bf16[7,1024,128]{2,1,0:T(8,128)(2,1)S(1)} %get-tuple-element.24.u_ref, ...), custom_call_target="tpu_custom_call" | custom-call | tf_op jit(solution)/shard_map/pallas_call | solution.py:483
  51.4 11.8 %all_to_all.21.recv_ref = bf16[8,64,256]{2,1,0:T(8,128)(2,1)S(1)} all-to-all(bf16[8,64,256]{2,1,0:T(8,128)(2,1)S(1)} %shard_map.110), channel_id=1, replica_groups=mesh['tiles'=8,'rhs'=4] {'tiles'}, dimensions={0} | all-to-all | bytes 524288 | tf_op jit(solution)/shard_map/all_to_all | solution.py:460
  63.1 0.0 copy-done.1
  63.1 2.2 %shard_map.111 = (bf16[64,1024]{1,0:T(8,128)(2,1)}, f32[32,1,256]{2,1,0:T(1,128)S(1)}) custom-call(s32[5,8]{1,0:T(8,128)S(4)} %get-tuple-element.22.plan_ref, bf16[8,64,256]{2,1,0:T(8,128)(2,1)S(1)} %all_to_all.21.recv_ref, bf16[64,1024]{1,0:T(8,128)(2,1)S(1)} %get-tuple-element.23.rhs_ref, bf16[7,1024,128]{2,1,0:T(8,128)(2,1)S(1)} %get-tuple-element.24.u_ref, ...), custom_call_target="tpu_custom_call" | custom-call | tf_op jit(solution)/shard_map/pallas_call | solution.py:494
  65.3 9.6 %all_to_all.22.parts_ref = f32[32,1,256]{2,1,0:T(1,128)S(1)} all-to-all(f32[32,1,256]{2,1,0:T(1,128)S(1)} %get-tuple-element.29), channel_id=1, replica_groups=mesh['tiles'=8,'rhs'=4] {'tiles','rhs'}, dimensions={0} | all-to-all | bytes 65536 | tf_op jit(solution)/shard_map/all_to_all | solution.py:505
  75.0 0.7 shard_map.112
Async XLA Ops:
  0.6 15.2 %collective-permute-start.4 = (bf16[1024,256]{1,0:T(8,128)(2,1)}, bf16[1024,256]{1,0:T(8,128)(2,1)S(1)}, u32[]{:S(2)}, u32[]{:S(2)}) collective-permute-start(bf16[1024,256]{1,0:T(8,128)(2,1)} %own_hbm.1), channel_id=1, source_target_pairs={{0,2},{1,3},{2,0},{3,1},{4,6},{5,7},{6,4},{7,5},{8,10},{9,11},{10,... | collective-permute-start | bytes 1572872 | tf_op jit(solution)/shard_map/ppermute | solution.py:119
  3.7 29.8 %collective-permute-start.3 = (bf16[1024,256]{1,0:T(8,128)(2,1)}, bf16[1024,256]{1,0:T(8,128)(2,1)S(1)}, u32[]{:S(2)}, u32[]{:S(2)}) collective-permute-start(bf16[1024,256]{1,0:T(8,128)(2,1)} %own_hbm.1), channel_id=1, source_target_pairs={{0,1},{1,0},{2,3},{3,2},{4,5},{5,4},{6,7},{7,6},{8,9},{9,8},{10,11... | collective-permute-start | bytes 1572872 | tf_op jit(solution)/shard_map/ppermute | solution.py:119
  15.8 18.7 %collective-permute-start.5 = (bf16[1024,256]{1,0:T(8,128)(2,1)S(1)}, bf16[1024,256]{1,0:T(8,128)(2,1)S(1)}, u32[]{:S(2)}, u32[]{:S(2)}) collective-permute-start(bf16[1024,256]{1,0:T(8,128)(2,1)S(1)} %collective-permute-done.4.refs_2_), channel_id=1, source_target_pairs={{0,1},{1,0},{2,3},{3,2},{4,5},{5,4},{6,7},{7,6},{8,9},{9,8},{10,11... | collective-permute-start | bytes 1572872 | tf_op jit(solution)/shard_map/ppermute | solution.py:119
  17.1 14.7 %all-to-all-start = ((s32[8,1,128]{2,1,0:T(1,128)}), s32[8,1,128]{2,1,0:T(1,128)S(1)}, u32[]{:S(2)}, u32[]{:S(2)}) async-start(s32[8,1,128]{2,1,0:T(1,128)} %get-tuple-element.20), calls=%async_computation | async-start | bytes 8192 | tf_op jit(solution)/shard_map/all_to_all | solution.py:408
  23.2 3.3 %collective-permute-start = (f32[9,32]{1,0:T(8,128)S(1)}, f32[9,32]{1,0:T(8,128)S(1)}, u32[]{:S(2)}, u32[]{:S(2)}) collective-permute-start(f32[9,32]{1,0:T(8,128)S(1)} %get-tuple-element.17.refs_0_), channel_id=1, source_target_pairs={{0,1},{1,0},{2,3},{3,2},{4,5},{5,4},{6,7},{7,6},{8,9},{9,8},{10,11... | collective-permute-start | bytes 3464 | tf_op jit(solution)/shard_map/ppermute | solution.py:119
  23.4 3.7 %collective-permute-start.1 = (f32[9,32]{1,0:T(8,128)S(1)}, f32[9,32]{1,0:T(8,128)S(1)}, u32[]{:S(2)}, u32[]{:S(2)}) collective-permute-start(f32[9,32]{1,0:T(8,128)S(1)} %get-tuple-element.17.refs_0_), channel_id=1, source_target_pairs={{0,2},{1,3},{2,0},{3,1},{4,6},{5,7},{6,4},{7,5},{8,10},{9,11},{10,... | collective-permute-start | bytes 3464 | tf_op jit(solution)/shard_map/ppermute | solution.py:119
  26.6 3.7 %collective-permute-start.2 = (f32[9,32]{1,0:T(8,128)S(1)}, f32[9,32]{1,0:T(8,128)S(1)}, u32[]{:S(2)}, u32[]{:S(2)}) collective-permute-start(f32[9,32]{1,0:T(8,128)S(1)} %collective-permute-done.refs_1_), channel_id=1, source_target_pairs={{0,2},{1,3},{2,0},{3,1},{4,6},{5,7},{6,4},{7,5},{8,10},{9,11},{10,... | collective-permute-start | bytes 3464 | tf_op jit(solution)/shard_map/ppermute | solution.py:119
  31.2 0.7 copy-start
  49.0 14.1 %copy-start.1 = (bf16[128,1024]{1,0:T(8,128)(2,1)S(1)}, bf16[128,1024]{1,0:T(8,128)(2,1)}, u32[]{:S(2)}) copy-start(bf16[128,1024]{1,0:T(8,128)(2,1)} %copy-done) | copy-start | bytes 786436

commit v4 on v3

--- a/solution.py
+++ b/solution.py
@@ -189,8 +189,7 @@
     wait_for(copies[2:])
 
 
-def cross_kernel(points_ref, *refs, amplitude, tiles_count):
-    cand_refs, cross_ref = refs[:-1], refs[-1]
+def cross_into(cross_ref, points_ref, cand_refs, amplitude, tiles_count):
     rhs_count = len(cand_refs)
     dims, group_len = points_ref.shape[0], cand_refs[0].shape[1]
     total = rhs_count * group_len
@@ -292,8 +291,10 @@
         )
 
 
-def early_kernel(plan_ref, rhs_ref, u_ref, v_ref, *refs, places):
-    inverse_refs, sums_ref = refs[:-1], refs[-1]
+def early_kernel(plan_ref, rhs_ref, u_ref, v_ref, points_ref, *refs, places, amplitude):
+    inverse_refs, refs = refs[: len(places)], refs[len(places) :]
+    cand_refs, (sums_ref, cross_ref) = refs[:-2], refs[-2:]
+    cross_into(cross_ref, points_ref, cand_refs, amplitude, plan_ref.shape[1])
     products = columns_product(plan_ref, rhs_ref, u_ref, v_ref, inverse_refs, places)
     for shift, product in products:
         sums_ref[shift - 1] = product
@@ -420,13 +421,6 @@
     cand = sent_far(packed)
     cand.update({d ^ 1: piece for d, piece in sent_far(beside).items()})
     amplitude = 4.0 / math.sqrt(block_len * tiles_count)
-    cross = pl.pallas_call(
-        functools.partial(cross_kernel, amplitude=amplitude, tiles_count=tiles_count),
-        out_shape=pltpu.VMEM((total, block_len), jnp.bfloat16),
-        in_specs=[VMEM] * (1 + rhs_count),
-        out_specs=VMEM,
-        compiler_params=PARAMS,
-    )(resident([points_kept])[0], *(cand[d] for d in range(rhs_count)))
     sent_on(inverse)
     plan, u_kept, own_piece = pl.pallas_call(
         plan_kernel,
@@ -444,7 +438,6 @@
             pltpu.SemaphoreType.DMA((4,)),
         ],
     )(told, in_hbm(tile_ranks), in_hbm(u_factors[0]), in_hbm(diag_inverse))
-    cross, plan = lax.optimization_barrier((cross, plan))
 
     plan = pltpu.with_memory_space_constraint(plan, pltpu.SMEM)
 
@@ -462,13 +455,17 @@
     late = [d for d in range(rhs_count) if d > 1 and d % 2]
     soon = [d for d in range(rhs_count) if d not in late]
     kept, pieces = weights()
-    sums = pl.pallas_call(
-        functools.partial(early_kernel, places=soon),
-        out_shape=pltpu.VMEM((tiles_count - 1, rows_here, 2 * width), jnp.float32),
-        in_specs=[SMEM] + [VMEM] * (3 + len(soon)),
-        out_specs=VMEM,
-        compiler_params=PARAMS,
-    )(plan, *kept, *(pieces[d] for d in soon))
+    given = [*resident([points_kept]), *(pieces[d] for d in soon)]
+    sums, cross = pl.pallas_call(
+        functools.partial(early_kernel, places=soon, amplitude=amplitude),
+        out_shape=(
+            pltpu.VMEM((tiles_count - 1, rows_here, 2 * width), jnp.float32),
+            pltpu.VMEM((total, block_len), jnp.bfloat16),
+        ),
+        in_specs=[SMEM] + [VMEM] * (4 + len(soon) + rhs_count),
+        out_specs=(VMEM, VMEM),
+        compiler_params=PARAMS,
+    )(plan, *kept, *given, *(cand[d] for d in range(rhs_count)))
     kept, pieces = weights()
     send = pl.pallas_call(
         functools.partial(first_kernel, places=late),

time: 76 us -> 75.2 us (0.989)
  waiting for transfers between devices: 15.3 us -> 14.1 us
    ppermute x6, waiting for transfers between devices: 15.3 us -> 12.1 us  [from_shard(): return lax.ppermute(piece, axis, xor_pairs(size, bit))]
    all_to_all x1, waiting for transfers between devices: 0.01 us -> 1.93 us  [dense_device(): told = lax.all_to_all(listed, 'tiles', 0, 0, tiled=True)]
    pallas_call x2 -> x1, Pallas kernels: 1.87 us -> 2.43 us  [dense_device(): pl.pallas_call(functools.partial(early_kernel, places=soon, amplitude=amp...]
  transfers between devices with their start and end apart: 7 -> 7, of which waited for: 2 -> 2; matrix products, arithmetic and copies ran while one was open for 0% -> 0% of each run, Pallas kernels for 8% -> 9%
where the time goes in v4:
time: 75.2 us; the launch traced here: 74.8 us
  blocking collectives  35.2 us (47%)
  waiting for transfers between devices  14.1 us (19%)
  Pallas kernels  12.8 us (17%)
  starting transfers between devices  11.4 us (15%)
    all_to_all x2, blocking collectives, exchange(): return lax.all_to_all(send, 'tiles', 0, 0, tiled=True)  25.5 us
    ppermute x6, waiting for transfers between devices, from_shard(): return lax.ppermute(piece, axis, xor_pairs(size, bit))  12.1 us
    all_to_all x1, blocking collectives, dense_device(): parts = lax.all_to_all(partial_values, ('tiles', 'rhs'), 0, 0, tiled=True)  9.74 us
    all_to_all x1, starting transfers between devices, dense_device(): told = lax.all_to_all(listed, 'tiles', 0, 0, tiled=True)  6.09 us
    ppermute x6, starting transfers between devices, from_shard(): return lax.ppermute(piece, axis, xor_pairs(size, bit))  5.29 us
    pallas_call x1, Pallas kernels, dense_device(): pl.pallas_call(functools.partial(early_kernel, places=soon, amplitude=amp...  2.43 us
    pallas_call x1, Pallas kernels, dense_device(): pl.pallas_call(middle_kernel, out_shape=sent, in_specs=[SMEM] + [VMEM] *...  2.36 us
    pallas_call x1, Pallas kernels, dense_device(): pl.pallas_call(last_kernel, out_shape=(rounded, pltpu.VMEM((devices, 1, o...  2.23 us
  transfers between devices with their start and end apart: 7, of which 2 were waited for; matrix products, arithmetic and copies ran while one was open for 0% of the time, Pallas kernels for 9%

profile of v4, /device:TPU:0, one launch (start us, length us, event | category | flops | bytes accessed | tf_op | source)
XLA Modules:
  0.0 74.8 jit_solution(18393838633934986152)
XLA Ops:
  0.6 3.0 %collective-permute-start.2 = (bf16[1024,256]{1,0:T(8,128)(2,1)}, bf16[1024,256]{1,0:T(8,128)(2,1)S(1)}, u32[]{:S(2)}, u32[]{:S(2)}) collective-permute-start(bf16[1024,256]{1,0:T(8,128)(2,1)} %own_hbm.1), channel_id=1, source_target_pairs={{0,2},{1,3},{2,0},{3,1},{4,6},{5,7},{6,4},{7,5},{8,10},{9,11},{10,... | collective-permute-start | bytes 1572872 | tf_op jit(solution)/shard_map/ppermute | solution.py:119
  3.7 0.0 collective-permute-start.1
  3.7 12.1 %collective-permute-done.2.refs_2_ = bf16[1024,256]{1,0:T(8,128)(2,1)S(1)} collective-permute-done((bf16[1024,256]{1,0:T(8,128)(2,1)}, bf16[1024,256]{1,0:T(8,128)(2,1)S(1)}, u32[]{:S(2)}, u32[]{:S(2)}) %collective-permute-start.2) | collective-permute-done | bytes 524320 | tf_op jit(solution)/shard_map/ppermute | solution.py:119
  15.8 0.0 collective-permute-start.5
  15.8 1.3 %shard_map.104 = (s32[8,1,128]{2,1,0:T(1,128)}, f32[9,32]{1,0:T(8,128)S(1)}) custom-call(f32[8,32]{1,0:T(8,128)} %cand_hbm.1, s32[1,32]{1,0:T(1,128)} %bitcast.5, s32[1,7]{1,0:T(1,128)} %rows_hbm.1), custom_call_target="tpu_custom_call" | custom-call | tf_op jit(solution)/shard_map/pallas_call | solution.py:392
  17.1 6.1 %all-to-all-start = ((s32[8,1,128]{2,1,0:T(1,128)}), s32[8,1,128]{2,1,0:T(1,128)S(1)}, u32[]{:S(2)}, u32[]{:S(2)}) async-start(s32[8,1,128]{2,1,0:T(1,128)} %get-tuple-element.16), calls=%async_computation | async-start | bytes 8192 | tf_op jit(solution)/shard_map/all_to_all | solution.py:409
  23.2 0.2 collective-permute-start
  23.4 1.5 %collective-permute-start.3 = (f32[9,32]{1,0:T(8,128)S(1)}, f32[9,32]{1,0:T(8,128)}, u32[]{:S(2)}, u32[]{:S(2)}) collective-permute-start(f32[9,32]{1,0:T(8,128)S(1)} %get-tuple-element.18.refs_3_), channel_id=1, source_target_pairs={{0,2},{1,3},{2,0},{3,1},{4,6},{5,7},{6,4},{7,5},{8,10},{9,11},{10,... | collective-permute-start | bytes 3464 | tf_op jit(solution)/shard_map/ppermute | solution.py:119
  24.9 1.6 %shard_map.106 = (bf16[64,1024]{1,0:T(8,128)(2,1)S(1)}, bf16[7,1024,128]{2,1,0:T(8,128)(2,1)S(1)}, f32[8,1024]{1,0:T(8,128)S(1)}) custom-call(bf16[64,1024]{1,0:T(8,128)(2,1)} %refs_0_.1, bf16[7,1024,128]{2,1,0:T(8,128)(2,1)} %bitcast.3, f32[8,1024]{1,0:T(8,128)} %refs_2_.1), custom_call_target="tpu_custom_call" | custom-call | tf_op jit(solution)/shard_map/pallas_call | solution.py:411
  26.5 0.0 copy-start
  26.6 0.6 copy-done
  27.2 0.0 collective-permute-done.refs_4_
  27.2 0.5 collective-permute-start.4
  27.7 1.9 %all-to-all-done.listed_in = s32[8,1,128]{2,1,0:T(1,128)S(1)} async-done(((s32[8,1,128]{2,1,0:T(1,128)}), s32[8,1,128]{2,1,0:T(1,128)S(1)}, u32[]{:S(2)}, u32[]{:S(2)}) %all-to-all-start) | async-done | bytes 4128 | tf_op jit(solution)/shard_map/all_to_all | solution.py:409
  29.6 0.0 copy-start.1
  29.6 1.6 %shard_map.105 = (s32[5,8]{1,0:T(8,128)S(4)}, bf16[7,1024,128]{2,1,0:T(8,128)(2,1)S(1)}, bf16[1024,256]{1,0:T(8,128)(2,1)S(1)}) custom-call(s32[8,1,128]{2,1,0:T(1,128)S(1)} %all-to-all-done.listed_in, s32[1,7]{1,0:T(1,128)} %ranks_hbm.1, bf16[7,1024,128]{2,1,0:T(8,128)(2,1)} %bitcast.4, bf16[1024,256]{1,0:T(8,128)(2,1)} %own_hbm.1), custom_call_target="tpu_custom_call" | custom-call | tf_op jit(solution)/shard_map/pallas_call | solution.py:425
  31.3 0.0 collective-permute-done.3.refs_5_
  31.3 0.0 collective-permute-done.4.refs_6_
  31.3 0.0 collective-permute-done.1.refs_1_
  31.3 0.0 copy-done.1
  31.3 2.4 %shard_map.107 = (f32[7,64,256]{2,1,0:T(8,128)S(1)}, bf16[128,1024]{1,0:T(8,128)(2,1)S(1)}) custom-call(s32[5,8]{1,0:T(8,128)S(4)} %get-tuple-element.17.plan_ref, bf16[64,1024]{1,0:T(8,128)(2,1)S(1)} %get-tuple-element.20.rhs_ref, bf16[7,1024,128]{2,1,0:T(8,128)(2,1)S(1)} %get-tuple-element.21.u_ref, bf16[7,1024,128]{2,1,0:T(8,128)(2,1)S(1)} %get-tuple-element.22.v_ref, ...), custom_call_target="tpu_custom_call" | custom-call | tf_op jit(solution)/shard_map/pallas_call | solution.py:459
  33.8 0.0 collective-permute-done.5.refs_0_.refs_3_
  33.8 0.6 shard_map.108
  34.4 13.7 %all_to_all.20.recv_ref = bf16[8,64,256]{2,1,0:T(8,128)(2,1)S(1)} all-to-all(bf16[8,64,256]{2,1,0:T(8,128)(2,1)S(1)} %shard_map.108), channel_id=1, replica_groups=mesh['tiles'=8,'rhs'=4] {'tiles'}, dimensions={0} | all-to-all | bytes 524288 | tf_op jit(solution)/shard_map/all_to_all | solution.py:453
  48.0 2.4 %shard_map.109 = bf16[8,64,256]{2,1,0:T(8,128)(2,1)S(1)} custom-call(s32[5,8]{1,0:T(8,128)S(4)} %get-tuple-element.17.plan_ref, bf16[8,64,256]{2,1,0:T(8,128)(2,1)S(1)} %all_to_all.20.recv_ref, bf16[64,1024]{1,0:T(8,128)(2,1)S(1)} %get-tuple-element.20.rhs_ref, bf16[7,1024,128]{2,1,0:T(8,128)(2,1)S(1)} %get-tuple-element.21.u_ref, ...), custom_call_target="tpu_custom_call" | custom-call | tf_op jit(solution)/shard_map/pallas_call | solution.py:480
  50.4 11.8 %all_to_all.21.recv_ref = bf16[8,64,256]{2,1,0:T(8,128)(2,1)S(1)} all-to-all(bf16[8,64,256]{2,1,0:T(8,128)(2,1)S(1)} %shard_map.109), channel_id=1, replica_groups=mesh['tiles'=8,'rhs'=4] {'tiles'}, dimensions={0} | all-to-all | bytes 524288 | tf_op jit(solution)/shard_map/all_to_all | solution.py:453
  62.2 2.2 %shard_map.110 = (bf16[64,1024]{1,0:T(8,128)(2,1)}, f32[32,1,256]{2,1,0:T(1,128)S(1)}) custom-call(s32[5,8]{1,0:T(8,128)S(4)} %get-tuple-element.17.plan_ref, bf16[8,64,256]{2,1,0:T(8,128)(2,1)S(1)} %all_to_all.21.recv_ref, bf16[64,1024]{1,0:T(8,128)(2,1)S(1)} %get-tuple-element.20.rhs_ref, bf16[7,1024,128]{2,1,0:T(8,128)(2,1)S(1)} %get-tuple-element.21.u_ref, ...), custom_call_target="tpu_custom_call" | custom-call | tf_op jit(solution)/shard_map/pallas_call | solution.py:491
  64.4 9.7 %all_to_all.22.parts_ref = f32[32,1,256]{2,1,0:T(1,128)S(1)} all-to-all(f32[32,1,256]{2,1,0:T(1,128)S(1)} %get-tuple-element.29), channel_id=1, replica_groups=mesh['tiles'=8,'rhs'=4] {'tiles','rhs'}, dimensions={0} | all-to-all | bytes 65536 | tf_op jit(solution)/shard_map/all_to_all | solution.py:502
  74.2 0.7 shard_map.111
Async XLA Ops:
  0.6 15.2 %collective-permute-start.2 = (bf16[1024,256]{1,0:T(8,128)(2,1)}, bf16[1024,256]{1,0:T(8,128)(2,1)S(1)}, u32[]{:S(2)}, u32[]{:S(2)}) collective-permute-start(bf16[1024,256]{1,0:T(8,128)(2,1)} %own_hbm.1), channel_id=1, source_target_pairs={{0,2},{1,3},{2,0},{3,1},{4,6},{5,7},{6,4},{7,5},{8,10},{9,11},{10,... | collective-permute-start | bytes 1572872 | tf_op jit(solution)/shard_map/ppermute | solution.py:119
  3.7 27.6 %collective-permute-start.1 = (bf16[1024,256]{1,0:T(8,128)(2,1)}, bf16[1024,256]{1,0:T(8,128)(2,1)S(1)}, u32[]{:S(2)}, u32[]{:S(2)}) collective-permute-start(bf16[1024,256]{1,0:T(8,128)(2,1)} %own_hbm.1), channel_id=1, source_target_pairs={{0,1},{1,0},{2,3},{3,2},{4,5},{5,4},{6,7},{7,6},{8,9},{9,8},{10,11... | collective-permute-start | bytes 1572872 | tf_op jit(solution)/shard_map/ppermute | solution.py:119
  15.8 18.0 %collective-permute-start.5 = (bf16[1024,256]{1,0:T(8,128)(2,1)S(1)}, bf16[1024,256]{1,0:T(8,128)(2,1)S(1)}, u32[]{:S(2)}, u32[]{:S(2)}) collective-permute-start(bf16[1024,256]{1,0:T(8,128)(2,1)S(1)} %collective-permute-done.2.refs_2_), channel_id=1, source_target_pairs={{0,1},{1,0},{2,3},{3,2},{4,5},{5,4},{6,7},{7,6},{8,9},{9,8},{10,11... | collective-permute-start | bytes 1572872 | tf_op jit(solution)/shard_map/ppermute | solution.py:119
  17.1 12.5 %all-to-all-start = ((s32[8,1,128]{2,1,0:T(1,128)}), s32[8,1,128]{2,1,0:T(1,128)S(1)}, u32[]{:S(2)}, u32[]{:S(2)}) async-start(s32[8,1,128]{2,1,0:T(1,128)} %get-tuple-element.16), calls=%async_computation | async-start | bytes 8192 | tf_op jit(solution)/shard_map/all_to_all | solution.py:409
  23.2 4.0 %collective-permute-start = (f32[9,32]{1,0:T(8,128)S(1)}, f32[9,32]{1,0:T(8,128)}, u32[]{:S(2)}, u32[]{:S(2)}) collective-permute-start(f32[9,32]{1,0:T(8,128)S(1)} %get-tuple-element.18.refs_3_), channel_id=1, source_target_pairs={{0,1},{1,0},{2,3},{3,2},{4,5},{5,4},{6,7},{7,6},{8,9},{9,8},{10,11... | collective-permute-start | bytes 3464 | tf_op jit(solution)/shard_map/ppermute | solution.py:119
  23.4 7.8 %collective-permute-start.3 = (f32[9,32]{1,0:T(8,128)S(1)}, f32[9,32]{1,0:T(8,128)}, u32[]{:S(2)}, u32[]{:S(2)}) collective-permute-start(f32[9,32]{1,0:T(8,128)S(1)} %get-tuple-element.18.refs_3_), channel_id=1, source_target_pairs={{0,2},{1,3},{2,0},{3,1},{4,6},{5,7},{6,4},{7,5},{8,10},{9,11},{10,... | collective-permute-start | bytes 3464 | tf_op jit(solution)/shard_map/ppermute | solution.py:119
  26.5 0.6 copy-start
  27.2 4.1 %collective-permute-start.4 = (f32[9,32]{1,0:T(8,128)}, f32[9,32]{1,0:T(8,128)}, u32[]{:S(2)}, u32[]{:S(2)}) collective-permute-start(f32[9,32]{1,0:T(8,128)} %collective-permute-done.refs_4_), channel_id=1, source_target_pairs={{0,2},{1,3},{2,0},{3,1},{4,6},{5,7},{6,4},{7,5},{8,10},{9,11},{10,... | collective-permute-start | bytes 3464 | tf_op jit(solution)/shard_map/ppermute | solution.py:119
  29.6 1.7 %copy-start.1 = (f32[8,1024]{1,0:T(8,128)S(1)}, f32[8,1024]{1,0:T(8,128)}, u32[]{:S(2)}) copy-start(f32[8,1024]{1,0:T(8,128)} %copy-done) | copy-start | bytes 98308
